TPU v7x, 32 devices: a whole 2x2x4 slice. The times are simulated.
32 devices in a mesh: group: 4 (over y, x), slot: 8 (over z, core).
Axes of the slice: x: 2, y: 2, z: 4, core: 2. Of those that a mesh axis runs over, the one named last changes fastest.
Arguments:
- tokens: bfloat16 [4096, 2048], P(('group', 'slot')), may hold values from -6 to 6
- cotangent: bfloat16 [4096, 512], P(('group', 'slot')), may hold values from -0.59765625 to 0.59765625
- weight_halves: bfloat16 [32, 1024, 512], P(('group', 'slot')), may hold values from -0.125 to 0.125
- momentum_halves: bfloat16 [32, 1024, 512], P(('group', 'slot')), may hold values from -6 to 6
- old_map: int32 [4, 4], replicated, may hold values from 0 to 3, each once within a row
- new_map: int32 [4, 8], replicated, may hold values from 0 to 3, as said below
- row_ids: int32 [32, 128], P(('group', 'slot')), may hold values from 0 to 127
Outputs:
- projected: bfloat16 [4096, 512], P(('group', 'slot'))
Inputs may be any that keep to these rules, and one draw needn't show every extreme that they name: `old_map`: each row names each of the group's experts once. `new_map`: every expert is hosted by one to four new slots; among the experts of every owner group one is hosted by exactly four.
All inputs are finite; a program needn't handle non-finite values.
Results may differ from a plain program's by a relative error of at most 0.007.
Values may be sent and summed in bfloat16 or wider, within the bound.
No kernel may reach another device: no remote copies, remote signals or barrier semaphores. Data moves between devices by JAX's collectives and lax.ppermute only.
A program may use at most 64 MiB of HBM per device.

v0:
```python
import functools
import math

import jax
import jax.numpy as jnp
from jax import lax
from jax.experimental import pallas as pl
from jax.experimental.pallas import tpu as pltpu
from jax.sharding import PartitionSpec as P


coef_a = 3.4445
coef_b = -4.775
coef_c = 2.0315
momentum_rate = 0.95
step_scale = 0.01
gram_eps = 1e-06
contract_rows = (((0,), (0,)), ((), ()))
STAGES = 2
MOST_PERMUTES = 4
LANES = 128
bf16 = jnp.bfloat16
f32 = jnp.float32


def shifted(shard, axis, stride, k):
    size = lax.axis_size(axis)
    return lax.ppermute(shard, axis, [(i, i ^ (k * stride)) for i in range(size)])


def swapped(shard):
    return shifted(shard, "slot", 1, 1)


def exchange(piece, axis, stride):
    size = lax.axis_size(axis)
    count = size // stride
    place = lax.axis_index(axis) // stride
    stacked = jnp.stack([piece(d) for d in range(count)])
    groups = [[first + stride * d for d in range(count)] for first in range(stride)]
    landed = lax.all_to_all(
        stacked,
        axis,
        split_axis=0,
        concat_axis=0,
        tiled=True,
        axis_index_groups=groups if stride > 1 else None,
    )
    return [lax.dynamic_index_in_dim(landed, place ^ k, 0, keepdims=False) for k in range(count)]


def pick_columns(token_block, which_half, slot_count):
    row_count, col_count = token_block.shape
    pieces_view = token_block.reshape(row_count, slot_count, 2, col_count // (2 * slot_count))
    chosen = lax.dynamic_index_in_dim(pieces_view, which_half, axis=2, keepdims=False)
    return chosen.reshape(row_count, col_count // 2)


def matmul(left, right):
    return jnp.dot(left.astype(bf16), right.astype(bf16), preferred_element_type=f32)


def tdot(left, right):
    return lax.dot_general(left, right, contract_rows, preferred_element_type=f32)


def update_matrix(gram):
    on_diagonal = lax.broadcasted_iota(jnp.int32, gram.shape, 0) == lax.broadcasted_iota(
        jnp.int32, gram.shape, 1
    )
    norm_sq = jnp.sum(jnp.where(on_diagonal, gram, 0.0), keepdims=True) + gram_eps
    first = gram * (1.0 / norm_sq)
    poly_first = coef_b * first + coef_c * matmul(first, first)
    half_way = coef_a * first + matmul(first, poly_first)
    second = coef_a * half_way + matmul(poly_first, half_way)
    poly_second = coef_b * second + coef_c * matmul(second, second)
    remainder = coef_a * (poly_first + poly_second) + matmul(poly_first, poly_second)
    return lax.rsqrt(norm_sq), remainder.astype(bf16)


def renew(weight, x0, x0_cols, factor, remainder, model_width):
    moved = coef_a * coef_a * x0_cols.astype(f32) + matmul(x0, remainder)
    scale = step_scale * math.sqrt(model_width) * factor
    return (weight.astype(f32) - scale * moved).astype(bf16)


def load_kernel(count, *refs):
    sources, targets, sems = refs[:count], refs[count : 2 * count], refs[2 * count]
    copies = [pltpu.make_async_copy(sources[i], targets[i], sems.at[i]) for i in range(count)]
    for copy in copies:
        copy.start()
    for copy in copies:
        copy.wait()


def own_place():
    slot = lax.axis_index("slot")
    return lax.axis_index("group"), lax.div(slot, 2), lax.rem(slot, 2)


def half_columns(ref, first, count, half):
    parts = []
    for j in range(count):
        start = (2 * (first + j) + half) * LANES
        parts.append(ref[:, pl.ds(pl.multiple_of(start, LANES), LANES)])
    return jnp.concatenate(parts, axis=1)


def front_kernel(own_ref, peer_ref, cot_ref, peer_cot_ref, momentum_ref, x0_ref, gram_ref):
    rows = x0_ref.shape[0]
    half = own_place()[2]
    cots = jnp.concatenate([cot_ref[...], peer_cot_ref[...]], axis=0)
    gram = None
    block = 2 * LANES
    for i in range(rows // block):
        toks = jnp.concatenate(
            [half_columns(ref, 2 * i, 2, half) for ref in (own_ref, peer_ref)], axis=0
        )
        part = slice(i * block, (i + 1) * block)
        x0 = momentum_rate * momentum_ref[part].astype(f32) + tdot(toks, cots)
        x0 = x0.astype(bf16)
        x0_ref[part] = x0
        term = tdot(x0, x0)
        gram = term if gram is None else gram + term
    gram_ref[...] = gram.astype(bf16)


def renew_pieces(model_width, stage, x0_ref, weight_ref, factor, remainder, out_refs):
    group = own_place()[0]
    chunk, width = out_refs[0].shape
    cols = slice(stage * width, (stage + 1) * width)
    for k in range(len(out_refs)):
        rows = pl.ds(pl.multiple_of((group ^ k) * chunk, chunk), chunk)
        out_refs[k][...] = renew(
            weight_ref[rows, cols],
            x0_ref[rows, :],
            x0_ref[rows, cols],
            factor,
            remainder,
            model_width,
        )


def update_kernel(model_width, own_ref, peer_ref, x0_ref, weight_ref, remainder_ref, factor_ref, *out_refs):
    gram = own_ref[...].astype(f32) + peer_ref[...].astype(f32)
    factor, remainder = update_matrix(gram)
    remainder_ref[...] = remainder
    factor_ref[...] = jnp.broadcast_to(factor, factor_ref.shape)
    width = out_refs[0].shape[1]
    renew_pieces(model_width, 0, x0_ref, weight_ref, factor, remainder[:, :width], out_refs)


def later_kernel(model_width, stage, remainder_ref, factor_ref, x0_ref, weight_ref, *out_refs):
    width = out_refs[0].shape[1]
    remainder = remainder_ref[:, stage * width : (stage + 1) * width]
    renew_pieces(
        model_width, stage, x0_ref, weight_ref, factor_ref[:1, :1], remainder, out_refs
    )


def choose_kernel(
    hosts, old_ref, new_ref, own_ref, peer_ref, ids_ref, peer_ids_ref, which_ref, *out_refs
):
    _, rows, chunk = out_refs[0].shape
    group, plane, half = own_place()
    planes = old_ref.shape[1]
    for k in range(len(out_refs)):
        for rel in range(2):
            wanted_slot = 2 * plane + (half ^ rel)
            owner = lax.div(wanted_slot, hosts)
            expert = new_ref[group ^ k, wanted_slot]
            holder = jnp.int32(0)
            for p in range(planes):
                holder = jnp.where(old_ref[owner, p] == expert, p, holder)
            which_ref[2 * k + rel] = plane ^ holder
    for rel, (ref, ids) in enumerate(((own_ref, ids_ref), (peer_ref, peer_ids_ref))):
        place = lax.broadcasted_iota(jnp.int32, (rows, rows), 0)
        pick = jnp.where(place == ids[...], 1.0, 0.0).astype(bf16)
        for k, out in enumerate(out_refs):
            count = chunk // LANES
            cols = half_columns(ref, (group ^ k) * count, count, half)
            out[rel] = tdot(pick, cols).astype(bf16)


def route_kernel(count, *refs):
    ins, outs, store = refs[:count], refs[count : 2 * count], refs[2 * count]
    group, plane, _ = own_place()
    for k in range(count):
        store[k] = ins[k][...]
    for k in range(count):
        outs[k][...] = store[group ^ plane ^ k]


def project_kernel(count, planes, which_ref, *refs):
    toks, weights = refs[:count], refs[count : count + planes]
    keep_ref, send_ref, store = refs[count + planes :]
    for k in range(planes):
        store[k] = weights[k][...]
    for rel in (1, 0):
        for k in range(count):
            got = jnp.dot(
                toks[k][rel], store[which_ref[2 * k + rel]], preferred_element_type=f32
            )
            if rel == 0:
                keep_ref[k] = got
            else:
                send_ref[k] = got.astype(bf16)


def join_kernel(count, keep_ref, other_ref, *out_refs):
    for k in range(count):
        out_refs[k][...] = (keep_ref[k] + other_ref[k].astype(f32)).astype(bf16)


def finish_kernel(count, *refs):
    out_ref = refs[-1]
    width = refs[0].shape[1]
    for stage in range(STAGES):
        parts = [r[...].astype(f32) for r in refs[stage * count : (stage + 1) * count]]
        out_ref[:, stage * width : (stage + 1) * width] = sum(parts).astype(out_ref.dtype)


VMEM, SMEM, HBM = pltpu.VMEM, pltpu.SMEM, pltpu.HBM


def call(kernel, arrays, outs, scratch=(), spaces=None, out_spaces=None):
    spaces = spaces or [VMEM] * len(arrays)
    out_spaces = out_spaces or [VMEM] * len(outs)
    made = {
        VMEM: lambda shape, dtype: pltpu.VMEM(shape, dtype),
        SMEM: lambda shape, dtype: pltpu.SMEM(shape, dtype),
        None: jax.ShapeDtypeStruct,
    }
    return pl.pallas_call(
        kernel,
        out_shape=[made[where](*out) for where, out in zip(out_spaces, outs)],
        in_specs=[pl.BlockSpec(memory_space=where or SMEM) for where in spaces],
        out_specs=[pl.BlockSpec(memory_space=where or VMEM) for where in out_spaces],
        scratch_shapes=list(scratch),
        compiler_params=pltpu.CompilerParams(vmem_limit_bytes=16 * 2**20),
    )(
        *[
            a if where is None else pltpu.with_memory_space_constraint(a, where)
            for where, a in zip(spaces, arrays)
        ]
    )


def on_device(tokens, cotangent, weight_halves, momentum_halves, old_map, new_map, row_ids):
    slot_count = lax.axis_size("slot")
    group_count = lax.axis_size("group")
    planes = slot_count // 2
    inputs = (
        tokens,
        cotangent,
        weight_halves[0],
        momentum_halves[0],
        old_map,
        new_map,
        row_ids,
    )
    fits = group_count == planes and planes <= MOST_PERMUTES
    if fits and tokens.shape[1] == 2 * slot_count * LANES:
        return by_permutes(*inputs)
    return by_all_to_all(*inputs)


FIRST = (3, 1, 2)
ACROSS = (3, 2, 1)


def spread(mine, axis, stride, order):
    landed = [mine[0]] + [None] * (len(mine) - 1)
    for k in order:
        if k < len(mine):
            landed[k] = shifted(mine[k], axis, stride, k)
    return landed


def by_permutes(tokens, cotangent, weight, momentum, old_map, new_map, row_ids):
    slot_count = lax.axis_size("slot")
    count = lax.axis_size("group")
    planes = slot_count // 2
    hosts = slot_count // count
    row_count, model_width = tokens.shape
    hidden = cotangent.shape[1]
    half_rows = model_width // 2
    chunk = half_rows // count
    width = hidden // STAGES

    peer_tokens = swapped(tokens)
    peer_cot = swapped(cotangent)
    to_load = [tokens, cotangent, momentum, weight, row_ids]
    tokens_in, cot_in, momentum_in, weight_in, ids_in = call(
        functools.partial(load_kernel, len(to_load)),
        to_load,
        [(a.shape, a.dtype) for a in to_load],
        [pltpu.SemaphoreType.DMA((len(to_load),))],
        spaces=[HBM] * len(to_load),
    )
    x0, own_gram = call(
        front_kernel,
        [tokens_in, peer_tokens, cot_in, peer_cot, momentum_in],
        [((half_rows, hidden), bf16), ((hidden, hidden), bf16)],
    )
    peer_gram = swapped(own_gram)
    peer_ids = swapped(row_ids)

    which, *token_cuts = call(
        functools.partial(choose_kernel, hosts),
        [old_map, new_map, tokens_in, peer_tokens, ids_in, peer_ids],
        [((2 * count,), jnp.int32)] + [((2, row_count, chunk), bf16)] * count,
        spaces=[None, None] + [VMEM] * 4,
        out_spaces=[SMEM] + [VMEM] * count,
    )

    remainder, factor, *first_pieces = call(
        functools.partial(update_kernel, model_width),
        [own_gram, peer_gram, x0, weight_in],
        [((hidden, hidden), bf16), ((8, LANES), f32)] + [((chunk, width), bf16)] * count,
    )
    arrived = []
    for stage in range(STAGES):
        pieces = first_pieces
        if stage:
            pieces = call(
                functools.partial(later_kernel, model_width, stage),
                [remainder, factor, x0, weight_in],
                [((chunk, width), bf16)] * count,
            )
        landed = spread(pieces, "group", 1, FIRST)
        routed = call(
            functools.partial(route_kernel, count),
            landed,
            [((chunk, width), bf16)] * count,
            [pltpu.VMEM((count, chunk, width), bf16)],
        )
        arrived.append(spread(routed, "slot", 2, ACROSS))

    requested = spread(token_cuts, "group", 1, FIRST)

    returned = []
    for stage in range(STAGES):
        keep, send = call(
            functools.partial(project_kernel, count, planes),
            [which] + requested + arrived[stage],
            [((count, row_count, width), f32), ((count, row_count, width), bf16)],
            [pltpu.VMEM((planes, chunk, width), bf16)],
            spaces=[SMEM] + [VMEM] * (count + planes),
        )
        other = swapped(send)
        mine = call(
            functools.partial(join_kernel, count),
            [keep, other],
            [((row_count, width), bf16)] * count,
        )
        returned += spread(mine, "group", 1, FIRST)
    return call(
        functools.partial(finish_kernel, count),
        returned,
        [((row_count, hidden), bf16)],
        out_spaces=[None],
    )[0]


def by_all_to_all(tokens, cotangent, weight, momentum, old_map, new_map, row_ids):
    slot_count = lax.axis_size("slot")
    group_count = lax.axis_size("group")
    planes = slot_count // 2
    owners = max(1, 2 * group_count // slot_count)
    row_count, model_width = tokens.shape
    hidden = cotangent.shape[1]
    half_rows = model_width // 2
    chunk = half_rows // group_count
    width = hidden // STAGES
    half = lax.axis_index("slot") % 2
    plane = lax.axis_index("slot") // 2
    group = lax.axis_index("group")
    hosts = slot_count // group_count

    from_group = group ^ jnp.arange(group_count)
    wanted_slot = 2 * plane + (half ^ jnp.arange(2))
    experts = new_map[from_group[:, None], wanted_slot[None, :]]
    lists = old_map[wanted_slot // hosts]
    holder = jnp.argmax((lists[None] == experts[:, :, None]).astype(jnp.int32), axis=2)

    peer_cot = swapped(cotangent)
    peer_tokens = swapped(pick_columns(tokens, 1 - half, slot_count))
    own_tokens = pick_columns(tokens, half, slot_count)
    gradient = tdot(own_tokens, cotangent) + tdot(peer_tokens, peer_cot)
    x0 = (momentum_rate * momentum.astype(f32) + gradient).astype(bf16)
    own_gram = tdot(x0, x0).astype(bf16)
    factor, remainder = update_matrix(own_gram.astype(f32) + swapped(own_gram).astype(f32))
    renewed = renew(weight, x0, x0, factor, remainder, model_width)

    pick = (row_ids[0][:, None] == jnp.arange(row_count)[None, :]).astype(bf16)
    chosen = jnp.dot(pick, tokens, preferred_element_type=f32).astype(bf16)
    own_chosen = pick_columns(chosen, half, slot_count)
    peer_chosen = swapped(pick_columns(chosen, 1 - half, slot_count))
    both = jnp.stack([own_chosen, peer_chosen]).reshape(2, row_count, group_count, chunk)
    requested = jnp.stack(exchange(lambda d: both[:, :, d], "group", 1))
    outputs = []
    for stage in range(STAGES):
        cols = slice(stage * width, (stage + 1) * width)
        chunks = renewed[:, cols].reshape(group_count, chunk, width)
        in_plane = jnp.stack(exchange(lambda d: chunks[d], "group", 1))
        by_owner = jnp.take(in_plane, group ^ jnp.arange(group_count), axis=0)
        by_plane = by_owner.reshape(planes, owners, chunk, width)
        arrived = jnp.stack(exchange(lambda d: by_plane[d], "slot", 2))
        partial = [
            jnp.einsum(
                "ktc,kcw->ktw",
                requested[:, rel],
                arrived[plane ^ holder[:, rel], (half ^ rel) * owners // 2],
                preferred_element_type=f32,
            )
            for rel in range(2)
        ]
        other = swapped(partial[1].astype(bf16))
        summed = (partial[0] + other.astype(f32)).astype(bf16)
        by_group = jnp.take(summed, group ^ jnp.arange(group_count), axis=0)
        returned = exchange(lambda d: by_group[d], "group", 1)
        outputs.append(sum(r.astype(f32) for r in returned).astype(bf16))
    return jnp.concatenate(outputs, axis=1)


def solution(mesh):
    placed = (
        P(("group", "slot"), None),
        P(("group", "slot"), None),
        P(("group", "slot"), None, None),
        P(("group", "slot"), None, None),
        P(),
        P(),
        P(("group", "slot"), None),
    )
    return jax.shard_map(
        on_device, mesh=mesh, in_specs=placed, out_specs=P(("group", "slot"), None), check_vma=False
    )
```

profile of v0, /device:TPU:0, one launch (start us, length us, event | category | flops | bytes accessed | tf_op | source)
XLA Modules:
  0.0 63.1 jit_solution(11905445789037744512)
XLA Ops:
  0.0 0.5 collective-permute-start
  0.5 0.0 collective-permute-start.5
  0.5 1.8 %shard_map.73 = (bf16[128,2048]{1,0:T(8,128)(2,1)S(1)}, bf16[128,512]{1,0:T(8,128)(2,1)S(1)}, bf16[1024,512]{1,0:T(8,128)(2,1)S(1)}, bf16[1024,512]{1,0:T(8,128)(2,1)S(1)}, s32[1,128]{1,0:T(1,128)S(1)}) custom-call(bf16[128,2048]{1,0:T(8,128)(2,1)} %refs_0_.1, bf16[128,512]{1,0:T(8,128)(2,1)} %refs_1_.1, bf16[1024,512]{1,0:T(8,128)(2,1)} %bitcast.2, ...), custom_call_target="tpu_custom_call" | custom-call | tf_op jit(solution)/shard_map/pallas_call | solution.py:234
  2.3 0.1 collective-permute-done.5.peer_cot_ref
  2.4 0.0 collective-permute-done.peer_ref
  2.4 1.6 %shard_map.75 = (bf16[1024,512]{1,0:T(8,128)(2,1)S(1)}, bf16[512,512]{1,0:T(8,128)(2,1)S(1)}) custom-call(bf16[128,2048]{1,0:T(8,128)(2,1)S(1)} %get-tuple-element.47.own_ref, bf16[128,2048]{1,0:T(8,128)(2,1)S(1)} %collective-permute-done.peer_ref, bf16[128,512]{1,0:T(8,128)(2,1)S(1)} %get-tuple-element.54.cot_ref, ...), custom_call_target="tpu_custom_call" | custom-call | tf_op jit(solution)/shard_map/pallas_call | solution.py:234
  4.0 0.5 collective-permute-start.6
  4.5 1.5 %collective-permute-done.6.peer_ref = bf16[512,512]{1,0:T(8,128)(2,1)S(1)} collective-permute-done((bf16[512,512]{1,0:T(8,128)(2,1)S(1)}, bf16[512,512]{1,0:T(8,128)(2,1)S(1)}, u32[]{:S(2)}, u32[]{:S(2)}) %collective-permute-start.6) | collective-permute-done | bytes 524320 | tf_op jit(solution)/shard_map/ppermute | solution.py:28
  6.0 2.5 %shard_map.76 = (bf16[512,512]{1,0:T(8,128)(2,1)S(1)}, f32[8,128]{1,0:T(8,128)S(1)}, bf16[256,256]{1,0:T(8,128)(2,1)S(1)}, bf16[256,256]{1,0:T(8,128)(2,1)S(1)},...) custom-call(bf16[512,512]{1,0:T(8,128)(2,1)S(1)} %get-tuple-element.56.own_ref, ...), custom_call_target="tpu_custom_call" | custom-call | tf_op jit(solution)/shard_map/pallas_call | solution.py:234
  8.5 0.5 shard_map.80
  9.0 0.0 copy-start.2
  9.0 2.9 %collective-permute-start.17 = (bf16[256,256]{1,0:T(8,128)(2,1)S(1)}, bf16[256,256]{1,0:T(8,128)(2,1)S(1)}, u32[]{:S(2)}, u32[]{:S(2)}) collective-permute-start(bf16[256,256]{1,0:T(8,128)(2,1)S(1)} %get-tuple-element.76), channel_id=1, source_target_pairs={{0,8},{8,0},{16,24},{24,16},{1,9},{9,1},{17,25},{25,17},{2,10},{10... | collective-permute-start | bytes 393224 | tf_op jit(solution)/shard_map/ppermute | solution.py:28
  12.0 1.5 %collective-permute-start.18 = (bf16[256,256]{1,0:T(8,128)(2,1)S(1)}, bf16[256,256]{1,0:T(8,128)(2,1)S(1)}, u32[]{:S(2)}, u32[]{:S(2)}) collective-permute-start(bf16[256,256]{1,0:T(8,128)(2,1)S(1)} %get-tuple-element.77), channel_id=1, source_target_pairs={{0,16},{8,24},{16,0},{24,8},{1,17},{9,25},{17,1},{25,9},{2,18},{10... | collective-permute-start | bytes 393224 | tf_op jit(solution)/shard_map/ppermute | solution.py:28
  13.5 0.0 collective-permute-start.1
  13.5 0.1 collective-permute-start.19
  13.6 1.0 %collective-permute-done.1.peer_ids_ref = s32[1,128]{1,0:T(1,128)S(1)} collective-permute-done((s32[1,128]{1,0:T(1,128)S(1)}, s32[1,128]{1,0:T(1,128)S(1)}, u32[]{:S(2)}, u32[]{:S(2)}) %collective-permute-start.1) | collective-permute-done | bytes 544 | tf_op jit(solution)/shard_map/ppermute | solution.py:28
  14.6 0.9 %shard_map.74 = (s32[8]{0:T(128)S(4)}, bf16[2,128,256]{2,1,0:T(8,128)(2,1)S(1)}, bf16[2,128,256]{2,1,0:T(8,128)(2,1)S(1)}, bf16[2,128,256]{2,1,0:T(8,128)(2,1)S(1)}, bf16[2,128,256]{2,1,0:T(8,128)(2,1)S(1)}) custom-call(s32[4,4]{1,0:T(4,128)S(1)} %copy-done, s32[4,8]{1,0:T(4,128)S(1)} %copy-done.1, bf16[128,2048]{1,0:T(8,128)(2,1)S(1)} %get-tuple-element.47.own_ref, ...), custom_call_target="tpu_custom_call" | custom-call | tf_op jit(solution)/shard_map/pallas_call | solution.py:234
  15.6 0.9 %collective-permute-start.2 = (bf16[2,128,256]{2,1,0:T(8,128)(2,1)S(1)}, bf16[2,128,256]{2,1,0:T(8,128)(2,1)S(1)}, u32[]{:S(2)}, u32[]{:S(2)}) collective-permute-start(bf16[2,128,256]{2,1,0:T(8,128)(2,1)S(1)} %get-tuple-element.51), channel_id=1, source_target_pairs={{0,8},{8,0},{16,24},{24,16},{1,9},{9,1},{17,25},{25,17},{2,10},{10... | collective-permute-start | bytes 393224 | tf_op jit(solution)/shard_map/ppermute | solution.py:28
  16.5 1.2 %collective-permute-start.7 = (bf16[256,256]{1,0:T(8,128)(2,1)S(1)}, bf16[256,256]{1,0:T(8,128)(2,1)S(1)}, u32[]{:S(2)}, u32[]{:S(2)}) collective-permute-start(bf16[256,256]{1,0:T(8,128)(2,1)S(1)} %get-tuple-element.60), channel_id=1, source_target_pairs={{0,8},{8,0},{16,24},{24,16},{1,9},{9,1},{17,25},{25,17},{2,10},{10... | collective-permute-start | bytes 393224 | tf_op jit(solution)/shard_map/ppermute | solution.py:28
  17.7 0.0 collective-permute-done.17.refs_1_
  17.7 0.8 %collective-permute-start.8 = (bf16[256,256]{1,0:T(8,128)(2,1)S(1)}, bf16[256,256]{1,0:T(8,128)(2,1)S(1)}, u32[]{:S(2)}, u32[]{:S(2)}) collective-permute-start(bf16[256,256]{1,0:T(8,128)(2,1)S(1)} %get-tuple-element.61), channel_id=1, source_target_pairs={{0,16},{8,24},{16,0},{24,8},{1,17},{9,25},{17,1},{25,9},{2,18},{10... | collective-permute-start | bytes 393224 | tf_op jit(solution)/shard_map/ppermute | solution.py:28
  18.5 0.9 %collective-permute-done.18.refs_2_ = bf16[256,256]{1,0:T(8,128)(2,1)S(1)} collective-permute-done((bf16[256,256]{1,0:T(8,128)(2,1)S(1)}, bf16[256,256]{1,0:T(8,128)(2,1)S(1)}, u32[]{:S(2)}, u32[]{:S(2)}) %collective-permute-start.18) | collective-permute-done | bytes 131104 | tf_op jit(solution)/shard_map/ppermute | solution.py:28
  19.4 1.7 %collective-permute-start.9 = (bf16[256,256]{1,0:T(8,128)(2,1)S(1)}, bf16[256,256]{1,0:T(8,128)(2,1)S(1)}, u32[]{:S(2)}, u32[]{:S(2)}) collective-permute-start(bf16[256,256]{1,0:T(8,128)(2,1)S(1)} %get-tuple-element.62), channel_id=1, source_target_pairs={{0,24},{8,16},{16,8},{24,0},{1,25},{9,17},{17,9},{25,1},{2,26},{10... | collective-permute-start | bytes 393224 | tf_op jit(solution)/shard_map/ppermute | solution.py:28
  21.1 0.0 collective-permute-done.19.refs_3_
  21.2 0.9 %collective-permute-start.3 = (bf16[2,128,256]{2,1,0:T(8,128)(2,1)S(1)}, bf16[2,128,256]{2,1,0:T(8,128)(2,1)S(1)}, u32[]{:S(2)}, u32[]{:S(2)}) collective-permute-start(bf16[2,128,256]{2,1,0:T(8,128)(2,1)S(1)} %get-tuple-element.52), channel_id=1, source_target_pairs={{0,16},{8,24},{16,0},{24,8},{1,17},{9,25},{17,1},{25,9},{2,18},{10... | collective-permute-start | bytes 393224 | tf_op jit(solution)/shard_map/ppermute | solution.py:28
  22.0 0.1 shard_map.81
  22.1 0.5 collective-permute-done.2.refs_1_
  22.7 2.5 %collective-permute-start.4 = (bf16[2,128,256]{2,1,0:T(8,128)(2,1)S(1)}, bf16[2,128,256]{2,1,0:T(8,128)(2,1)S(1)}, u32[]{:S(2)}, u32[]{:S(2)}) collective-permute-start(bf16[2,128,256]{2,1,0:T(8,128)(2,1)S(1)} %get-tuple-element.53), channel_id=1, source_target_pairs={{0,24},{8,16},{16,8},{24,0},{1,25},{9,17},{17,9},{25,1},{2,26},{10... | collective-permute-start | bytes 393224 | tf_op jit(solution)/shard_map/ppermute | solution.py:28
  25.1 0.3 collective-permute-done.7.refs_1_
  25.5 1.6 %collective-permute-start.20 = (bf16[256,256]{1,0:T(8,128)(2,1)S(1)}, bf16[256,256]{1,0:T(8,128)(2,1)S(1)}, u32[]{:S(2)}, u32[]{:S(2)}) collective-permute-start(bf16[256,256]{1,0:T(8,128)(2,1)S(1)} %get-tuple-element.80), channel_id=1, source_target_pairs={{0,2},{1,3},{2,0},{3,1},{4,6},{5,7},{6,4},{7,5},{8,10},{9,11},{10,... | collective-permute-start | bytes 393224 | tf_op jit(solution)/shard_map/ppermute | solution.py:28
  27.0 0.0 collective-permute-done.8.refs_2_
  27.0 2.6 %collective-permute-start.21 = (bf16[256,256]{1,0:T(8,128)(2,1)S(1)}, bf16[256,256]{1,0:T(8,128)(2,1)S(1)}, u32[]{:S(2)}, u32[]{:S(2)}) collective-permute-start(bf16[256,256]{1,0:T(8,128)(2,1)S(1)} %get-tuple-element.81), channel_id=1, source_target_pairs={{0,4},{1,5},{2,6},{3,7},{4,0},{5,1},{6,2},{7,3},{8,12},{9,13},{10,... | collective-permute-start | bytes 393224 | tf_op jit(solution)/shard_map/ppermute | solution.py:28
  29.6 0.0 collective-permute-done.9.refs_3_
  29.6 3.2 %collective-permute-start.22 = (bf16[256,256]{1,0:T(8,128)(2,1)S(1)}, bf16[256,256]{1,0:T(8,128)(2,1)S(1)}, u32[]{:S(2)}, u32[]{:S(2)}) collective-permute-start(bf16[256,256]{1,0:T(8,128)(2,1)S(1)} %get-tuple-element.82), channel_id=1, source_target_pairs={{0,6},{1,7},{2,4},{3,5},{4,2},{5,3},{6,0},{7,1},{8,14},{9,15},{10,... | collective-permute-start | bytes 393224 | tf_op jit(solution)/shard_map/ppermute | solution.py:28
  32.9 0.1 shard_map.77
  33.0 0.0 collective-permute-done.3.refs_2_
  33.0 0.6 collective-permute-start.10
  33.5 0.0 collective-permute-done.4.refs_3_
  33.5 2.6 %collective-permute-start.11 = (bf16[256,256]{1,0:T(8,128)(2,1)S(1)}, bf16[256,256]{1,0:T(8,128)(2,1)S(1)}, u32[]{:S(2)}, u32[]{:S(2)}) collective-permute-start(bf16[256,256]{1,0:T(8,128)(2,1)S(1)} %get-tuple-element.65), channel_id=1, source_target_pairs={{0,4},{1,5},{2,6},{3,7},{4,0},{5,1},{6,2},{7,3},{8,12},{9,13},{10,... | collective-permute-start | bytes 393224 | tf_op jit(solution)/shard_map/ppermute | solution.py:28
  36.1 0.0 collective-permute-done.20.refs_5_
  36.1 1.3 %collective-permute-start.12 = (bf16[256,256]{1,0:T(8,128)(2,1)S(1)}, bf16[256,256]{1,0:T(8,128)(2,1)S(1)}, u32[]{:S(2)}, u32[]{:S(2)}) collective-permute-start(bf16[256,256]{1,0:T(8,128)(2,1)S(1)} %get-tuple-element.66), channel_id=1, source_target_pairs={{0,6},{1,7},{2,4},{3,5},{4,2},{5,3},{6,0},{7,1},{8,14},{9,15},{10,... | collective-permute-start | bytes 393224 | tf_op jit(solution)/shard_map/ppermute | solution.py:28
  37.4 1.2 %collective-permute-done.21.refs_6_ = bf16[256,256]{1,0:T(8,128)(2,1)S(1)} collective-permute-done((bf16[256,256]{1,0:T(8,128)(2,1)S(1)}, bf16[256,256]{1,0:T(8,128)(2,1)S(1)}, u32[]{:S(2)}, u32[]{:S(2)}) %collective-permute-start.21) | collective-permute-done | bytes 131104 | tf_op jit(solution)/shard_map/ppermute | solution.py:28
  38.6 0.8 %collective-permute-done.22.refs_7_ = bf16[256,256]{1,0:T(8,128)(2,1)S(1)} collective-permute-done((bf16[256,256]{1,0:T(8,128)(2,1)S(1)}, bf16[256,256]{1,0:T(8,128)(2,1)S(1)}, u32[]{:S(2)}, u32[]{:S(2)}) %collective-permute-start.22) | collective-permute-done | bytes 131104 | tf_op jit(solution)/shard_map/ppermute | solution.py:28
  39.5 0.3 shard_map.82
  39.8 0.1 collective-permute-start.23
  39.9 0.2 collective-permute-done.10.refs_5_
  40.1 10.2 %collective-permute-done.11.refs_6_ = bf16[256,256]{1,0:T(8,128)(2,1)S(1)} collective-permute-done((bf16[256,256]{1,0:T(8,128)(2,1)S(1)}, bf16[256,256]{1,0:T(8,128)(2,1)S(1)}, u32[]{:S(2)}, u32[]{:S(2)}) %collective-permute-start.11) | collective-permute-done | bytes 131104 | tf_op jit(solution)/shard_map/ppermute | solution.py:28
  50.3 0.0 collective-permute-done.12.refs_7_
  50.3 0.3 shard_map.78
  50.6 0.1 collective-permute-start.13
  50.7 0.0 collective-permute-done.23.other_ref
  50.8 1.0 %collective-permute-start.24 = (bf16[128,256]{1,0:T(8,128)(2,1)S(1)}, bf16[128,256]{1,0:T(8,128)(2,1)S(1)}, u32[]{:S(2)}, u32[]{:S(2)}) collective-permute-start(bf16[128,256]{1,0:T(8,128)(2,1)S(1)} %get-tuple-element.86), channel_id=1, source_target_pairs={{0,8},{8,0},{16,24},{24,16},{1,9},{9,1},{17,25},{25,17},{2,10},{10... | collective-permute-start | bytes 196616 | tf_op jit(solution)/shard_map/ppermute | solution.py:28
  51.8 1.8 %collective-permute-start.25 = (bf16[128,256]{1,0:T(8,128)(2,1)S(1)}, bf16[128,256]{1,0:T(8,128)(2,1)S(1)}, u32[]{:S(2)}, u32[]{:S(2)}) collective-permute-start(bf16[128,256]{1,0:T(8,128)(2,1)S(1)} %get-tuple-element.87), channel_id=1, source_target_pairs={{0,16},{8,24},{16,0},{24,8},{1,17},{9,25},{17,1},{25,9},{2,18},{10... | collective-permute-start | bytes 196616 | tf_op jit(solution)/shard_map/ppermute | solution.py:28
  53.6 0.8 %collective-permute-start.26 = (bf16[128,256]{1,0:T(8,128)(2,1)S(1)}, bf16[128,256]{1,0:T(8,128)(2,1)S(1)}, u32[]{:S(2)}, u32[]{:S(2)}) collective-permute-start(bf16[128,256]{1,0:T(8,128)(2,1)S(1)} %get-tuple-element.88), channel_id=1, source_target_pairs={{0,24},{8,16},{16,8},{24,0},{1,25},{9,17},{17,9},{25,1},{2,26},{10... | collective-permute-start | bytes 196616 | tf_op jit(solution)/shard_map/ppermute | solution.py:28
  54.3 0.0 collective-permute-done.13.other_ref
  54.4 1.0 %collective-permute-start.14 = (bf16[128,256]{1,0:T(8,128)(2,1)S(1)}, bf16[128,256]{1,0:T(8,128)(2,1)S(1)}, u32[]{:S(2)}, u32[]{:S(2)}) collective-permute-start(bf16[128,256]{1,0:T(8,128)(2,1)S(1)} %get-tuple-element.70), channel_id=1, source_target_pairs={{0,8},{8,0},{16,24},{24,16},{1,9},{9,1},{17,25},{25,17},{2,10},{10... | collective-permute-start | bytes 196616 | tf_op jit(solution)/shard_map/ppermute | solution.py:28
  55.4 1.8 %collective-permute-start.15 = (bf16[128,256]{1,0:T(8,128)(2,1)S(1)}, bf16[128,256]{1,0:T(8,128)(2,1)S(1)}, u32[]{:S(2)}, u32[]{:S(2)}) collective-permute-start(bf16[128,256]{1,0:T(8,128)(2,1)S(1)} %get-tuple-element.71), channel_id=1, source_target_pairs={{0,16},{8,24},{16,0},{24,8},{1,17},{9,25},{17,1},{25,9},{2,18},{10... | collective-permute-start | bytes 196616 | tf_op jit(solution)/shard_map/ppermute | solution.py:28
  57.2 0.0 collective-permute-done.24.refs_5_
  57.2 0.8 %collective-permute-start.16 = (bf16[128,256]{1,0:T(8,128)(2,1)S(1)}, bf16[128,256]{1,0:T(8,128)(2,1)S(1)}, u32[]{:S(2)}, u32[]{:S(2)}) collective-permute-start(bf16[128,256]{1,0:T(8,128)(2,1)S(1)} %get-tuple-element.72), channel_id=1, source_target_pairs={{0,24},{8,16},{16,8},{24,0},{1,25},{9,17},{17,9},{25,1},{2,26},{10... | collective-permute-start | bytes 196616 | tf_op jit(solution)/shard_map/ppermute | solution.py:28
  58.0 1.3 %collective-permute-done.26.refs_7_ = bf16[128,256]{1,0:T(8,128)(2,1)S(1)} collective-permute-done((bf16[128,256]{1,0:T(8,128)(2,1)S(1)}, bf16[128,256]{1,0:T(8,128)(2,1)S(1)}, u32[]{:S(2)}, u32[]{:S(2)}) %collective-permute-start.26) | collective-permute-done | bytes 65568 | tf_op jit(solution)/shard_map/ppermute | solution.py:28
  59.3 0.0 collective-permute-done.14.refs_1_
  59.3 0.8 %collective-permute-done.15.refs_2_ = bf16[128,256]{1,0:T(8,128)(2,1)S(1)} collective-permute-done((bf16[128,256]{1,0:T(8,128)(2,1)S(1)}, bf16[128,256]{1,0:T(8,128)(2,1)S(1)}, u32[]{:S(2)}, u32[]{:S(2)}) %collective-permute-start.15) | collective-permute-done | bytes 65568 | tf_op jit(solution)/shard_map/ppermute | solution.py:28
  60.1 2.3 %collective-permute-done.16.refs_3_ = bf16[128,256]{1,0:T(8,128)(2,1)S(1)} collective-permute-done((bf16[128,256]{1,0:T(8,128)(2,1)S(1)}, bf16[128,256]{1,0:T(8,128)(2,1)S(1)}, u32[]{:S(2)}, u32[]{:S(2)}) %collective-permute-start.16) | collective-permute-done | bytes 65568 | tf_op jit(solution)/shard_map/ppermute | solution.py:28
  62.4 0.7 %shard_map.84 = bf16[128,512]{1,0:T(8,128)(2,1)} custom-call(bf16[128,256]{1,0:T(8,128)(2,1)S(1)} %get-tuple-element.69.refs_0_, bf16[128,256]{1,0:T(8,128)(2,1)S(1)} %collective-permute-done.14.refs_1_, bf16[128,256]{1,0:T(8,128)(2,1)S(1)} %collective-permute-done.15.refs_2_, bf16[128,256]{1,0:T(8,128)(2,1)S(1)} %collective-permute-done.16.refs_3_, ...), custom_call_target="tpu_custom_call" | custom-call | tf_op jit(solution)/shard_map/pallas_call | solution.py:234
  (8 shorter events, 0.1 us)
Async XLA Ops:
  0.0 2.4 %collective-permute-start = (bf16[128,2048]{1,0:T(8,128)(2,1)}, bf16[128,2048]{1,0:T(8,128)(2,1)S(1)}, u32[]{:S(2)}, u32[]{:S(2)}) collective-permute-start(bf16[128,2048]{1,0:T(8,128)(2,1)} %refs_0_.1), channel_id=1, source_target_pairs={{0,1},{1,0},{2,3},{3,2},{4,5},{5,4},{6,7},{7,6},{8,9},{9,8},{10,11... | collective-permute-start | bytes 1572872 | tf_op jit(solution)/shard_map/ppermute | solution.py:28
  0.5 1.9 %collective-permute-start.5 = (bf16[128,512]{1,0:T(8,128)(2,1)}, bf16[128,512]{1,0:T(8,128)(2,1)S(1)}, u32[]{:S(2)}, u32[]{:S(2)}) collective-permute-start(bf16[128,512]{1,0:T(8,128)(2,1)} %refs_1_.1), channel_id=1, source_target_pairs={{0,1},{1,0},{2,3},{3,2},{4,5},{5,4},{6,7},{7,6},{8,9},{9,8},{10,11... | collective-permute-start | bytes 393224 | tf_op jit(solution)/shard_map/ppermute | solution.py:28
  4.0 2.0 %collective-permute-start.6 = (bf16[512,512]{1,0:T(8,128)(2,1)S(1)}, bf16[512,512]{1,0:T(8,128)(2,1)S(1)}, u32[]{:S(2)}, u32[]{:S(2)}) collective-permute-start(bf16[512,512]{1,0:T(8,128)(2,1)S(1)} %get-tuple-element.56.own_ref), channel_id=1, source_target_pairs={{0,1},{1,0},{2,3},{3,2},{4,5},{5,4},{6,7},{7,6},{8,9},{9,8},{10,11... | collective-permute-start | bytes 1572872 | tf_op jit(solution)/shard_map/ppermute | solution.py:28
  9.0 4.4 %copy-start.2 = (s32[1,128]{1,0:T(1,128)S(1)}, s32[1,128]{1,0:T(1,128)}, u32[]{:S(2)}) copy-start(s32[1,128]{1,0:T(1,128)} %refs_4_.1) | copy-start | bytes 1540
  9.0 8.7 %collective-permute-start.17 = (bf16[256,256]{1,0:T(8,128)(2,1)S(1)}, bf16[256,256]{1,0:T(8,128)(2,1)S(1)}, u32[]{:S(2)}, u32[]{:S(2)}) collective-permute-start(bf16[256,256]{1,0:T(8,128)(2,1)S(1)} %get-tuple-element.76), channel_id=1, source_target_pairs={{0,8},{8,0},{16,24},{24,16},{1,9},{9,1},{17,25},{25,17},{2,10},{10... | collective-permute-start | bytes 393224 | tf_op jit(solution)/shard_map/ppermute | solution.py:28
  12.0 2.7 %copy-start.1 = (s32[4,8]{1,0:T(4,128)S(1)}, s32[4,8]{1,0:T(4,128)}, u32[]{:S(2)}) copy-start(s32[4,8]{1,0:T(4,128)} %new_ref.1) | copy-start | bytes 388
  12.0 2.7 %copy-start = (s32[4,4]{1,0:T(4,128)S(1)}, s32[4,4]{1,0:T(4,128)}, u32[]{:S(2)}) copy-start(s32[4,4]{1,0:T(4,128)} %old_ref.1) | copy-start | bytes 196
  12.0 7.5 %collective-permute-start.18 = (bf16[256,256]{1,0:T(8,128)(2,1)S(1)}, bf16[256,256]{1,0:T(8,128)(2,1)S(1)}, u32[]{:S(2)}, u32[]{:S(2)}) collective-permute-start(bf16[256,256]{1,0:T(8,128)(2,1)S(1)} %get-tuple-element.77), channel_id=1, source_target_pairs={{0,16},{8,24},{16,0},{24,8},{1,17},{9,25},{17,1},{25,9},{2,18},{10... | collective-permute-start | bytes 393224 | tf_op jit(solution)/shard_map/ppermute | solution.py:28
  13.5 1.2 %collective-permute-start.1 = (s32[1,128]{1,0:T(1,128)S(1)}, s32[1,128]{1,0:T(1,128)S(1)}, u32[]{:S(2)}, u32[]{:S(2)}) collective-permute-start(s32[1,128]{1,0:T(1,128)S(1)} %copy-done.2), channel_id=1, source_target_pairs={{0,1},{1,0},{2,3},{3,2},{4,5},{5,4},{6,7},{7,6},{8,9},{9,8},{10,11... | collective-permute-start | bytes 1544 | tf_op jit(solution)/shard_map/ppermute | solution.py:28
  13.5 7.7 %collective-permute-start.19 = (bf16[256,256]{1,0:T(8,128)(2,1)S(1)}, bf16[256,256]{1,0:T(8,128)(2,1)S(1)}, u32[]{:S(2)}, u32[]{:S(2)}) collective-permute-start(bf16[256,256]{1,0:T(8,128)(2,1)S(1)} %get-tuple-element.78), channel_id=1, source_target_pairs={{0,24},{8,16},{16,8},{24,0},{1,25},{9,17},{17,9},{25,1},{2,26},{10... | collective-permute-start | bytes 393224 | tf_op jit(solution)/shard_map/ppermute | solution.py:28
  15.6 7.0 %collective-permute-start.2 = (bf16[2,128,256]{2,1,0:T(8,128)(2,1)S(1)}, bf16[2,128,256]{2,1,0:T(8,128)(2,1)S(1)}, u32[]{:S(2)}, u32[]{:S(2)}) collective-permute-start(bf16[2,128,256]{2,1,0:T(8,128)(2,1)S(1)} %get-tuple-element.51), channel_id=1, source_target_pairs={{0,8},{8,0},{16,24},{24,16},{1,9},{9,1},{17,25},{25,17},{2,10},{10... | collective-permute-start | bytes 393224 | tf_op jit(solution)/shard_map/ppermute | solution.py:28
  16.5 9.0 %collective-permute-start.7 = (bf16[256,256]{1,0:T(8,128)(2,1)S(1)}, bf16[256,256]{1,0:T(8,128)(2,1)S(1)}, u32[]{:S(2)}, u32[]{:S(2)}) collective-permute-start(bf16[256,256]{1,0:T(8,128)(2,1)S(1)} %get-tuple-element.60), channel_id=1, source_target_pairs={{0,8},{8,0},{16,24},{24,16},{1,9},{9,1},{17,25},{25,17},{2,10},{10... | collective-permute-start | bytes 393224 | tf_op jit(solution)/shard_map/ppermute | solution.py:28
  17.7 9.3 %collective-permute-start.8 = (bf16[256,256]{1,0:T(8,128)(2,1)S(1)}, bf16[256,256]{1,0:T(8,128)(2,1)S(1)}, u32[]{:S(2)}, u32[]{:S(2)}) collective-permute-start(bf16[256,256]{1,0:T(8,128)(2,1)S(1)} %get-tuple-element.61), channel_id=1, source_target_pairs={{0,16},{8,24},{16,0},{24,8},{1,17},{9,25},{17,1},{25,9},{2,18},{10... | collective-permute-start | bytes 393224 | tf_op jit(solution)/shard_map/ppermute | solution.py:28
  19.4 10.2 %collective-permute-start.9 = (bf16[256,256]{1,0:T(8,128)(2,1)S(1)}, bf16[256,256]{1,0:T(8,128)(2,1)S(1)}, u32[]{:S(2)}, u32[]{:S(2)}) collective-permute-start(bf16[256,256]{1,0:T(8,128)(2,1)S(1)} %get-tuple-element.62), channel_id=1, source_target_pairs={{0,24},{8,16},{16,8},{24,0},{1,25},{9,17},{17,9},{25,1},{2,26},{10... | collective-permute-start | bytes 393224 | tf_op jit(solution)/shard_map/ppermute | solution.py:28
  21.2 11.8 %collective-permute-start.3 = (bf16[2,128,256]{2,1,0:T(8,128)(2,1)S(1)}, bf16[2,128,256]{2,1,0:T(8,128)(2,1)S(1)}, u32[]{:S(2)}, u32[]{:S(2)}) collective-permute-start(bf16[2,128,256]{2,1,0:T(8,128)(2,1)S(1)} %get-tuple-element.52), channel_id=1, source_target_pairs={{0,16},{8,24},{16,0},{24,8},{1,17},{9,25},{17,1},{25,9},{2,18},{10... | collective-permute-start | bytes 393224 | tf_op jit(solution)/shard_map/ppermute | solution.py:28
  22.7 10.9 %collective-permute-start.4 = (bf16[2,128,256]{2,1,0:T(8,128)(2,1)S(1)}, bf16[2,128,256]{2,1,0:T(8,128)(2,1)S(1)}, u32[]{:S(2)}, u32[]{:S(2)}) collective-permute-start(bf16[2,128,256]{2,1,0:T(8,128)(2,1)S(1)} %get-tuple-element.53), channel_id=1, source_target_pairs={{0,24},{8,16},{16,8},{24,0},{1,25},{9,17},{17,9},{25,1},{2,26},{10... | collective-permute-start | bytes 393224 | tf_op jit(solution)/shard_map/ppermute | solution.py:28
  25.5 10.6 %collective-permute-start.20 = (bf16[256,256]{1,0:T(8,128)(2,1)S(1)}, bf16[256,256]{1,0:T(8,128)(2,1)S(1)}, u32[]{:S(2)}, u32[]{:S(2)}) collective-permute-start(bf16[256,256]{1,0:T(8,128)(2,1)S(1)} %get-tuple-element.80), channel_id=1, source_target_pairs={{0,2},{1,3},{2,0},{3,1},{4,6},{5,7},{6,4},{7,5},{8,10},{9,11},{10,... | collective-permute-start | bytes 393224 | tf_op jit(solution)/shard_map/ppermute | solution.py:28
  27.0 11.6 %collective-permute-start.21 = (bf16[256,256]{1,0:T(8,128)(2,1)S(1)}, bf16[256,256]{1,0:T(8,128)(2,1)S(1)}, u32[]{:S(2)}, u32[]{:S(2)}) collective-permute-start(bf16[256,256]{1,0:T(8,128)(2,1)S(1)} %get-tuple-element.81), channel_id=1, source_target_pairs={{0,4},{1,5},{2,6},{3,7},{4,0},{5,1},{6,2},{7,3},{8,12},{9,13},{10,... | collective-permute-start | bytes 393224 | tf_op jit(solution)/shard_map/ppermute | solution.py:28
  29.6 9.8 %collective-permute-start.22 = (bf16[256,256]{1,0:T(8,128)(2,1)S(1)}, bf16[256,256]{1,0:T(8,128)(2,1)S(1)}, u32[]{:S(2)}, u32[]{:S(2)}) collective-permute-start(bf16[256,256]{1,0:T(8,128)(2,1)S(1)} %get-tuple-element.82), channel_id=1, source_target_pairs={{0,6},{1,7},{2,4},{3,5},{4,2},{5,3},{6,0},{7,1},{8,14},{9,15},{10,... | collective-permute-start | bytes 393224 | tf_op jit(solution)/shard_map/ppermute | solution.py:28
  33.0 7.1 %collective-permute-start.10 = (bf16[256,256]{1,0:T(8,128)(2,1)S(1)}, bf16[256,256]{1,0:T(8,128)(2,1)S(1)}, u32[]{:S(2)}, u32[]{:S(2)}) collective-permute-start(bf16[256,256]{1,0:T(8,128)(2,1)S(1)} %get-tuple-element.64), channel_id=1, source_target_pairs={{0,2},{1,3},{2,0},{3,1},{4,6},{5,7},{6,4},{7,5},{8,10},{9,11},{10,... | collective-permute-start | bytes 393224 | tf_op jit(solution)/shard_map/ppermute | solution.py:28
  33.5 16.8 %collective-permute-start.11 = (bf16[256,256]{1,0:T(8,128)(2,1)S(1)}, bf16[256,256]{1,0:T(8,128)(2,1)S(1)}, u32[]{:S(2)}, u32[]{:S(2)}) collective-permute-start(bf16[256,256]{1,0:T(8,128)(2,1)S(1)} %get-tuple-element.65), channel_id=1, source_target_pairs={{0,4},{1,5},{2,6},{3,7},{4,0},{5,1},{6,2},{7,3},{8,12},{9,13},{10,... | collective-permute-start | bytes 393224 | tf_op jit(solution)/shard_map/ppermute | solution.py:28
  36.1 14.2 %collective-permute-start.12 = (bf16[256,256]{1,0:T(8,128)(2,1)S(1)}, bf16[256,256]{1,0:T(8,128)(2,1)S(1)}, u32[]{:S(2)}, u32[]{:S(2)}) collective-permute-start(bf16[256,256]{1,0:T(8,128)(2,1)S(1)} %get-tuple-element.66), channel_id=1, source_target_pairs={{0,6},{1,7},{2,4},{3,5},{4,2},{5,3},{6,0},{7,1},{8,14},{9,15},{10,... | collective-permute-start | bytes 393224 | tf_op jit(solution)/shard_map/ppermute | solution.py:28
  39.8 10.9 %collective-permute-start.23 = (bf16[4,128,256]{2,1,0:T(8,128)(2,1)S(1)}, bf16[4,128,256]{2,1,0:T(8,128)(2,1)S(1)}, u32[]{:S(2)}, u32[]{:S(2)}) collective-permute-start(bf16[4,128,256]{2,1,0:T(8,128)(2,1)S(1)} %get-tuple-element.84), channel_id=1, source_target_pairs={{0,1},{1,0},{2,3},{3,2},{4,5},{5,4},{6,7},{7,6},{8,9},{9,8},{10,11... | collective-permute-start | bytes 786440 | tf_op jit(solution)/shard_map/ppermute | solution.py:28
  50.6 3.7 %collective-permute-start.13 = (bf16[4,128,256]{2,1,0:T(8,128)(2,1)S(1)}, bf16[4,128,256]{2,1,0:T(8,128)(2,1)S(1)}, u32[]{:S(2)}, u32[]{:S(2)}) collective-permute-start(bf16[4,128,256]{2,1,0:T(8,128)(2,1)S(1)} %get-tuple-element.68), channel_id=1, source_target_pairs={{0,1},{1,0},{2,3},{3,2},{4,5},{5,4},{6,7},{7,6},{8,9},{9,8},{10,11... | collective-permute-start | bytes 786440 | tf_op jit(solution)/shard_map/ppermute | solution.py:28
  50.8 6.4 %collective-permute-start.24 = (bf16[128,256]{1,0:T(8,128)(2,1)S(1)}, bf16[128,256]{1,0:T(8,128)(2,1)S(1)}, u32[]{:S(2)}, u32[]{:S(2)}) collective-permute-start(bf16[128,256]{1,0:T(8,128)(2,1)S(1)} %get-tuple-element.86), channel_id=1, source_target_pairs={{0,8},{8,0},{16,24},{24,16},{1,9},{9,1},{17,25},{25,17},{2,10},{10... | collective-permute-start | bytes 196616 | tf_op jit(solution)/shard_map/ppermute | solution.py:28
  51.8 6.1 %collective-permute-start.25 = (bf16[128,256]{1,0:T(8,128)(2,1)S(1)}, bf16[128,256]{1,0:T(8,128)(2,1)S(1)}, u32[]{:S(2)}, u32[]{:S(2)}) collective-permute-start(bf16[128,256]{1,0:T(8,128)(2,1)S(1)} %get-tuple-element.87), channel_id=1, source_target_pairs={{0,16},{8,24},{16,0},{24,8},{1,17},{9,25},{17,1},{25,9},{2,18},{10... | collective-permute-start | bytes 196616 | tf_op jit(solution)/shard_map/ppermute | solution.py:28
  53.6 5.7 %collective-permute-start.26 = (bf16[128,256]{1,0:T(8,128)(2,1)S(1)}, bf16[128,256]{1,0:T(8,128)(2,1)S(1)}, u32[]{:S(2)}, u32[]{:S(2)}) collective-permute-start(bf16[128,256]{1,0:T(8,128)(2,1)S(1)} %get-tuple-element.88), channel_id=1, source_target_pairs={{0,24},{8,16},{16,8},{24,0},{1,25},{9,17},{17,9},{25,1},{2,26},{10... | collective-permute-start | bytes 196616 | tf_op jit(solution)/shard_map/ppermute | solution.py:28
  54.4 4.9 %collective-permute-start.14 = (bf16[128,256]{1,0:T(8,128)(2,1)S(1)}, bf16[128,256]{1,0:T(8,128)(2,1)S(1)}, u32[]{:S(2)}, u32[]{:S(2)}) collective-permute-start(bf16[128,256]{1,0:T(8,128)(2,1)S(1)} %get-tuple-element.70), channel_id=1, source_target_pairs={{0,8},{8,0},{16,24},{24,16},{1,9},{9,1},{17,25},{25,17},{2,10},{10... | collective-permute-start | bytes 196616 | tf_op jit(solution)/shard_map/ppermute | solution.py:28
  55.4 4.6 %collective-permute-start.15 = (bf16[128,256]{1,0:T(8,128)(2,1)S(1)}, bf16[128,256]{1,0:T(8,128)(2,1)S(1)}, u32[]{:S(2)}, u32[]{:S(2)}) collective-permute-start(bf16[128,256]{1,0:T(8,128)(2,1)S(1)} %get-tuple-element.71), channel_id=1, source_target_pairs={{0,16},{8,24},{16,0},{24,8},{1,17},{9,25},{17,1},{25,9},{2,18},{10... | collective-permute-start | bytes 196616 | tf_op jit(solution)/shard_map/ppermute | solution.py:28
  57.2 5.2 %collective-permute-start.16 = (bf16[128,256]{1,0:T(8,128)(2,1)S(1)}, bf16[128,256]{1,0:T(8,128)(2,1)S(1)}, u32[]{:S(2)}, u32[]{:S(2)}) collective-permute-start(bf16[128,256]{1,0:T(8,128)(2,1)S(1)} %get-tuple-element.72), channel_id=1, source_target_pairs={{0,24},{8,16},{16,8},{24,0},{1,25},{9,17},{17,9},{25,1},{2,26},{10... | collective-permute-start | bytes 196616 | tf_op jit(solution)/shard_map/ppermute | solution.py:28
where the time goes:
time: 63.2 us; the launch traced here: 63.1 us
  starting transfers between devices  32.7 us (52%)
  waiting for transfers between devices  21.3 us (34%)
  Pallas kernels  8.95 us (14%)
    ppermute x27, starting transfers between devices, shifted(): return lax.ppermute(shard, axis, [(i, i ^ k * stride) for i in range(size)])  32.7 us
    ppermute x27, waiting for transfers between devices, shifted(): return lax.ppermute(shard, axis, [(i, i ^ k * stride) for i in range(size)])  21.3 us
    pallas_call x12, Pallas kernels, call(): pl.pallas_call(kernel, out_shape=[made[where](*out) for where, out in zip...  8.95 us
  transfers between devices with their start and end apart: 27, of which 13 were waited for; matrix products, arithmetic and copies ran while one was open for 0% of the time, Pallas kernels for 6%

commit v1 on v0

--- a/solution.py
+++ b/solution.py
@@ -16,7 +16,8 @@
 step_scale = 0.01
 gram_eps = 1e-06
 contract_rows = (((0,), (0,)), ((), ()))
-STAGES = 2
+WIDTHS = (1, 2, 1)
+TAILS = ((0, 1), (2,))
 MOST_PERMUTES = 4
 LANES = 128
 bf16 = jnp.bfloat16
@@ -125,10 +126,15 @@
     gram_ref[...] = gram.astype(bf16)
 
 
-def renew_pieces(model_width, stage, x0_ref, weight_ref, factor, remainder, out_refs):
+def stage_columns(hidden):
+    unit = hidden // sum(WIDTHS)
+    starts = [unit * sum(WIDTHS[:i]) for i in range(len(WIDTHS))]
+    return [slice(start, start + unit * share) for start, share in zip(starts, WIDTHS)]
+
+
+def renew_pieces(model_width, cols, x0_ref, weight_ref, factor, remainder, out_refs):
     group = own_place()[0]
-    chunk, width = out_refs[0].shape
-    cols = slice(stage * width, (stage + 1) * width)
+    chunk = out_refs[0].shape[0]
     for k in range(len(out_refs)):
         rows = pl.ds(pl.multiple_of((group ^ k) * chunk, chunk), chunk)
         out_refs[k][...] = renew(
@@ -141,21 +147,19 @@
         )
 
 
-def update_kernel(model_width, own_ref, peer_ref, x0_ref, weight_ref, remainder_ref, factor_ref, *out_refs):
+def update_kernel(
+    model_width, cols, own_ref, peer_ref, x0_ref, weight_ref, remainder_ref, factor_ref, *out_refs
+):
     gram = own_ref[...].astype(f32) + peer_ref[...].astype(f32)
     factor, remainder = update_matrix(gram)
     remainder_ref[...] = remainder
     factor_ref[...] = jnp.broadcast_to(factor, factor_ref.shape)
-    width = out_refs[0].shape[1]
-    renew_pieces(model_width, 0, x0_ref, weight_ref, factor, remainder[:, :width], out_refs)
-
-
-def later_kernel(model_width, stage, remainder_ref, factor_ref, x0_ref, weight_ref, *out_refs):
-    width = out_refs[0].shape[1]
-    remainder = remainder_ref[:, stage * width : (stage + 1) * width]
-    renew_pieces(
-        model_width, stage, x0_ref, weight_ref, factor_ref[:1, :1], remainder, out_refs
-    )
+    renew_pieces(model_width, cols, x0_ref, weight_ref, factor, remainder[:, cols], out_refs)
+
+
+def later_kernel(model_width, cols, remainder_ref, factor_ref, x0_ref, weight_ref, *out_refs):
+    remainder = remainder_ref[:, cols]
+    renew_pieces(model_width, cols, x0_ref, weight_ref, factor_ref[:1, :1], remainder, out_refs)
 
 
 def choose_kernel(
@@ -191,20 +195,25 @@
         outs[k][...] = store[group ^ plane ^ k]
 
 
-def project_kernel(count, planes, which_ref, *refs):
-    toks, weights = refs[:count], refs[count : count + planes]
-    keep_ref, send_ref, store = refs[count + planes :]
-    for k in range(planes):
-        store[k] = weights[k][...]
+def project_kernel(count, planes, stages, which_ref, *refs):
+    toks, weights = refs[:count], refs[count : count + planes * stages]
+    keep_ref, send_ref = refs[count + planes * stages :][:2]
+    stores = refs[count + planes * stages + 2 :]
+    for stage in range(stages):
+        for k in range(planes):
+            stores[stage][k] = weights[stage * planes + k][...]
     for rel in (1, 0):
         for k in range(count):
-            got = jnp.dot(
-                toks[k][rel], store[which_ref[2 * k + rel]], preferred_element_type=f32
-            )
-            if rel == 0:
-                keep_ref[k] = got
-            else:
-                send_ref[k] = got.astype(bf16)
+            place = which_ref[2 * k + rel]
+            start = 0
+            for store in stores:
+                cols = slice(start, start + store.shape[2])
+                start = cols.stop
+                got = jnp.dot(toks[k][rel], store[place], preferred_element_type=f32)
+                if rel == 0:
+                    keep_ref[k, :, cols] = got
+                else:
+                    send_ref[k, :, cols] = got.astype(bf16)
 
 
 def join_kernel(count, keep_ref, other_ref, *out_refs):
@@ -214,10 +223,12 @@
 
 def finish_kernel(count, *refs):
     out_ref = refs[-1]
-    width = refs[0].shape[1]
-    for stage in range(STAGES):
-        parts = [r[...].astype(f32) for r in refs[stage * count : (stage + 1) * count]]
-        out_ref[:, stage * width : (stage + 1) * width] = sum(parts).astype(out_ref.dtype)
+    start = 0
+    for tail in range(len(TAILS)):
+        mine = refs[tail * count : (tail + 1) * count]
+        cols = slice(start, start + mine[0].shape[1])
+        start = cols.stop
+        out_ref[:, cols] = sum(r[...].astype(f32) for r in mine).astype(out_ref.dtype)
 
 
 VMEM, SMEM, HBM = pltpu.VMEM, pltpu.SMEM, pltpu.HBM
@@ -286,10 +297,11 @@
     hidden = cotangent.shape[1]
     half_rows = model_width // 2
     chunk = half_rows // count
-    width = hidden // STAGES
+    columns = stage_columns(hidden)
 
     peer_tokens = swapped(tokens)
     peer_cot = swapped(cotangent)
+    peer_ids = swapped(row_ids)
     to_load = [tokens, cotangent, momentum, weight, row_ids]
     tokens_in, cot_in, momentum_in, weight_in, ids_in = call(
         functools.partial(load_kernel, len(to_load)),
@@ -304,7 +316,6 @@
         [((half_rows, hidden), bf16), ((hidden, hidden), bf16)],
     )
     peer_gram = swapped(own_gram)
-    peer_ids = swapped(row_ids)
 
     which, *token_cuts = call(
         functools.partial(choose_kernel, hosts),
@@ -314,17 +325,18 @@
         out_spaces=[SMEM] + [VMEM] * count,
     )
 
-    remainder, factor, *first_pieces = call(
-        functools.partial(update_kernel, model_width),
-        [own_gram, peer_gram, x0, weight_in],
-        [((hidden, hidden), bf16), ((8, LANES), f32)] + [((chunk, width), bf16)] * count,
-    )
     arrived = []
-    for stage in range(STAGES):
-        pieces = first_pieces
-        if stage:
+    for stage, cols in enumerate(columns):
+        width = cols.stop - cols.start
+        if stage == 0:
+            remainder, factor, *pieces = call(
+                functools.partial(update_kernel, model_width, cols),
+                [own_gram, peer_gram, x0, weight_in],
+                [((hidden, hidden), bf16), ((8, LANES), f32)] + [((chunk, width), bf16)] * count,
+            )
+        else:
             pieces = call(
-                functools.partial(later_kernel, model_width, stage),
+                functools.partial(later_kernel, model_width, cols),
                 [remainder, factor, x0, weight_in],
                 [((chunk, width), bf16)] * count,
             )
@@ -340,19 +352,20 @@
     requested = spread(token_cuts, "group", 1, FIRST)
 
     returned = []
-    for stage in range(STAGES):
+    for stages in TAILS:
+        widths = [columns[i].stop - columns[i].start for i in stages]
         keep, send = call(
-            functools.partial(project_kernel, count, planes),
-            [which] + requested + arrived[stage],
-            [((count, row_count, width), f32), ((count, row_count, width), bf16)],
-            [pltpu.VMEM((planes, chunk, width), bf16)],
-            spaces=[SMEM] + [VMEM] * (count + planes),
+            functools.partial(project_kernel, count, planes, len(stages)),
+            [which] + requested + sum((arrived[i] for i in stages), []),
+            [((count, row_count, sum(widths)), f32), ((count, row_count, sum(widths)), bf16)],
+            [pltpu.VMEM((planes, chunk, width), bf16) for width in widths],
+            spaces=[SMEM] + [VMEM] * (count + planes * len(stages)),
         )
         other = swapped(send)
         mine = call(
             functools.partial(join_kernel, count),
             [keep, other],
-            [((row_count, width), bf16)] * count,
+            [((row_count, sum(widths)), bf16)] * count,
         )
         returned += spread(mine, "group", 1, FIRST)
     return call(
@@ -372,7 +385,6 @@
     hidden = cotangent.shape[1]
     half_rows = model_width // 2
     chunk = half_rows // group_count
-    width = hidden // STAGES
     half = lax.axis_index("slot") % 2
     plane = lax.axis_index("slot") // 2
     group = lax.axis_index("group")
@@ -400,8 +412,8 @@
     both = jnp.stack([own_chosen, peer_chosen]).reshape(2, row_count, group_count, chunk)
     requested = jnp.stack(exchange(lambda d: both[:, :, d], "group", 1))
     outputs = []
-    for stage in range(STAGES):
-        cols = slice(stage * width, (stage + 1) * width)
+    for cols in (slice(0, hidden // 2), slice(hidden // 2, hidden)):
+        width = cols.stop - cols.start
         chunks = renewed[:, cols].reshape(group_count, chunk, width)
         in_plane = jnp.stack(exchange(lambda d: chunks[d], "group", 1))
         by_owner = jnp.take(in_plane, group ^ jnp.arange(group_count), axis=0)

time: 63.2 us -> 79 us (1.25)
  waiting for transfers between devices: 21.3 us -> 31.3 us
  starting transfers between devices: 32.7 us -> 37.9 us
    ppermute x27 -> x33, waiting for transfers between devices: 21.3 us -> 31.3 us  [shifted(): return lax.ppermute(shard, axis, [(i, i ^ k * stride) for i in range(size)])]
    ppermute x27 -> x33, starting transfers between devices: 32.7 us -> 37.9 us  [shifted(): return lax.ppermute(shard, axis, [(i, i ^ k * stride) for i in range(size)])]
    pallas_call x12 -> x14, Pallas kernels: 8.95 us -> 9.45 us  [call(): pl.pallas_call(kernel, out_shape=[made[where](*out) for where, out in zip...]
  transfers between devices with their start and end apart: 27 -> 33, of which waited for: 13 -> 13; matrix products, arithmetic and copies ran while one was open for 0% -> 0% of each run, Pallas kernels for 6% -> 5%
where the time goes in v1:
time: 79 us; the launch traced here: 78.8 us
  starting transfers between devices  37.9 us (48%)
  waiting for transfers between devices  31.3 us (40%)
  Pallas kernels  9.45 us (12%)
    ppermute x33, starting transfers between devices, shifted(): return lax.ppermute(shard, axis, [(i, i ^ k * stride) for i in range(size)])  37.9 us
    ppermute x33, waiting for transfers between devices, shifted(): return lax.ppermute(shard, axis, [(i, i ^ k * stride) for i in range(size)])  31.3 us
    pallas_call x14, Pallas kernels, call(): pl.pallas_call(kernel, out_shape=[made[where](*out) for where, out in zip...  9.45 us
  transfers between devices with their start and end apart: 33, of which 13 were waited for; matrix products, arithmetic and copies ran while one was open for 0% of the time, Pallas kernels for 5%

profile of v1, /device:TPU:0, one launch (start us, length us, event | category | flops | bytes accessed | tf_op | source)
XLA Modules:
  0.0 78.8 jit_solution(9568855856420661967)
XLA Ops:
  0.0 0.5 collective-permute-start
  0.5 0.0 collective-permute-start.5
  0.5 1.8 %shard_map.73 = (bf16[128,2048]{1,0:T(8,128)(2,1)S(1)}, bf16[128,512]{1,0:T(8,128)(2,1)S(1)}, bf16[1024,512]{1,0:T(8,128)(2,1)S(1)}, bf16[1024,512]{1,0:T(8,128)(2,1)S(1)}, s32[1,128]{1,0:T(1,128)S(1)}) custom-call(bf16[128,2048]{1,0:T(8,128)(2,1)} %refs_0_.1, bf16[128,512]{1,0:T(8,128)(2,1)} %refs_1_.1, bf16[1024,512]{1,0:T(8,128)(2,1)} %bitcast.2, ...), custom_call_target="tpu_custom_call" | custom-call | tf_op jit(solution)/shard_map/pallas_call | solution.py:245
  2.3 0.1 collective-permute-done.5.peer_cot_ref
  2.4 0.0 collective-permute-done.peer_ref
  2.4 1.5 %shard_map.75 = (bf16[1024,512]{1,0:T(8,128)(2,1)S(1)}, bf16[512,512]{1,0:T(8,128)(2,1)S(1)}) custom-call(bf16[128,2048]{1,0:T(8,128)(2,1)S(1)} %get-tuple-element.55.own_ref, bf16[128,2048]{1,0:T(8,128)(2,1)S(1)} %collective-permute-done.peer_ref, bf16[128,512]{1,0:T(8,128)(2,1)S(1)} %get-tuple-element.62.cot_ref, ...), custom_call_target="tpu_custom_call" | custom-call | tf_op jit(solution)/shard_map/pallas_call | solution.py:245
  4.0 0.5 collective-permute-start.6
  4.5 1.5 %collective-permute-done.6.peer_ref = bf16[512,512]{1,0:T(8,128)(2,1)S(1)} collective-permute-done((bf16[512,512]{1,0:T(8,128)(2,1)S(1)}, bf16[512,512]{1,0:T(8,128)(2,1)S(1)}, u32[]{:S(2)}, u32[]{:S(2)}) %collective-permute-start.6) | collective-permute-done | bytes 524320 | tf_op jit(solution)/shard_map/ppermute | solution.py:29
  6.0 2.5 %shard_map.76 = (bf16[512,512]{1,0:T(8,128)(2,1)S(1)}, f32[8,128]{1,0:T(8,128)S(1)}, bf16[256,128]{1,0:T(8,128)(2,1)S(1)}, bf16[256,128]{1,0:T(8,128)(2,1)S(1)},...) custom-call(bf16[512,512]{1,0:T(8,128)(2,1)S(1)} %get-tuple-element.64.own_ref, ...), custom_call_target="tpu_custom_call" | custom-call | tf_op jit(solution)/shard_map/pallas_call | solution.py:245
  8.5 2.9 %collective-permute-start.7 = (bf16[256,128]{1,0:T(8,128)(2,1)S(1)}, bf16[256,128]{1,0:T(8,128)(2,1)S(1)}, u32[]{:S(2)}, u32[]{:S(2)}) collective-permute-start(bf16[256,128]{1,0:T(8,128)(2,1)S(1)} %get-tuple-element.68), channel_id=1, source_target_pairs={{0,8},{8,0},{16,24},{24,16},{1,9},{9,1},{17,25},{25,17},{2,10},{10... | collective-permute-start | bytes 196616 | tf_op jit(solution)/shard_map/ppermute | solution.py:29
  11.4 0.5 shard_map.78
  11.9 0.1 collective-permute-start.13
  12.0 2.0 %collective-permute-start.8 = (bf16[256,128]{1,0:T(8,128)(2,1)S(1)}, bf16[256,128]{1,0:T(8,128)(2,1)S(1)}, u32[]{:S(2)}, u32[]{:S(2)}) collective-permute-start(bf16[256,128]{1,0:T(8,128)(2,1)S(1)} %get-tuple-element.69), channel_id=1, source_target_pairs={{0,16},{8,24},{16,0},{24,8},{1,17},{9,25},{17,1},{25,9},{2,18},{10... | collective-permute-start | bytes 196616 | tf_op jit(solution)/shard_map/ppermute | solution.py:29
  14.0 1.4 %collective-permute-start.9 = (bf16[256,128]{1,0:T(8,128)(2,1)S(1)}, bf16[256,128]{1,0:T(8,128)(2,1)S(1)}, u32[]{:S(2)}, u32[]{:S(2)}) collective-permute-start(bf16[256,128]{1,0:T(8,128)(2,1)S(1)} %get-tuple-element.70), channel_id=1, source_target_pairs={{0,24},{8,16},{16,8},{24,0},{1,25},{9,17},{17,9},{25,1},{2,26},{10... | collective-permute-start | bytes 196616 | tf_op jit(solution)/shard_map/ppermute | solution.py:29
  15.4 0.0 collective-permute-start.1
  15.4 1.2 %collective-permute-done.1.peer_ids_ref = s32[1,128]{1,0:T(1,128)S(1)} collective-permute-done((s32[1,128]{1,0:T(1,128)S(1)}, s32[1,128]{1,0:T(1,128)S(1)}, u32[]{:S(2)}, u32[]{:S(2)}) %collective-permute-start.1) | collective-permute-done | bytes 544 | tf_op jit(solution)/shard_map/ppermute | solution.py:29
  16.6 1.5 %collective-permute-start.14 = (bf16[256,256]{1,0:T(8,128)(2,1)S(1)}, bf16[256,256]{1,0:T(8,128)(2,1)S(1)}, u32[]{:S(2)}, u32[]{:S(2)}) collective-permute-start(bf16[256,256]{1,0:T(8,128)(2,1)S(1)} %get-tuple-element.79), channel_id=1, source_target_pairs={{0,16},{8,24},{16,0},{24,8},{1,17},{9,25},{17,1},{25,9},{2,18},{10... | collective-permute-start | bytes 393224 | tf_op jit(solution)/shard_map/ppermute | solution.py:29
  18.1 0.0 collective-permute-start.15
  18.2 0.9 %shard_map.74 = (s32[8]{0:T(128)S(4)}, bf16[2,128,256]{2,1,0:T(8,128)(2,1)S(1)}, bf16[2,128,256]{2,1,0:T(8,128)(2,1)S(1)}, bf16[2,128,256]{2,1,0:T(8,128)(2,1)S(1)}, bf16[2,128,256]{2,1,0:T(8,128)(2,1)S(1)}) custom-call(s32[4,4]{1,0:T(4,128)S(1)} %copy-done, s32[4,8]{1,0:T(4,128)S(1)} %copy-done.1, bf16[128,2048]{1,0:T(8,128)(2,1)S(1)} %get-tuple-element.55.own_ref, ...), custom_call_target="tpu_custom_call" | custom-call | tf_op jit(solution)/shard_map/pallas_call | solution.py:245
  19.1 0.0 collective-permute-done.8.refs_2_
  19.1 2.0 %collective-permute-start.2 = (bf16[2,128,256]{2,1,0:T(8,128)(2,1)S(1)}, bf16[2,128,256]{2,1,0:T(8,128)(2,1)S(1)}, u32[]{:S(2)}, u32[]{:S(2)}) collective-permute-start(bf16[2,128,256]{2,1,0:T(8,128)(2,1)S(1)} %get-tuple-element.59), channel_id=1, source_target_pairs={{0,8},{8,0},{16,24},{24,16},{1,9},{9,1},{17,25},{25,17},{2,10},{10... | collective-permute-start | bytes 393224 | tf_op jit(solution)/shard_map/ppermute | solution.py:29
  21.1 0.0 collective-permute-done.9.refs_3_
  21.1 1.5 %collective-permute-start.3 = (bf16[2,128,256]{2,1,0:T(8,128)(2,1)S(1)}, bf16[2,128,256]{2,1,0:T(8,128)(2,1)S(1)}, u32[]{:S(2)}, u32[]{:S(2)}) collective-permute-start(bf16[2,128,256]{2,1,0:T(8,128)(2,1)S(1)} %get-tuple-element.60), channel_id=1, source_target_pairs={{0,16},{8,24},{16,0},{24,8},{1,17},{9,25},{17,1},{25,9},{2,18},{10... | collective-permute-start | bytes 393224 | tf_op jit(solution)/shard_map/ppermute | solution.py:29
  22.6 0.0 collective-permute-start.4
  22.7 3.0 %collective-permute-done.14.refs_2_ = bf16[256,256]{1,0:T(8,128)(2,1)S(1)} collective-permute-done((bf16[256,256]{1,0:T(8,128)(2,1)S(1)}, bf16[256,256]{1,0:T(8,128)(2,1)S(1)}, u32[]{:S(2)}, u32[]{:S(2)}) %collective-permute-start.14) | collective-permute-done | bytes 131104 | tf_op jit(solution)/shard_map/ppermute | solution.py:29
  25.8 1.6 %collective-permute-start.10 = (bf16[256,128]{1,0:T(8,128)(2,1)S(1)}, bf16[256,128]{1,0:T(8,128)(2,1)S(1)}, u32[]{:S(2)}, u32[]{:S(2)}) collective-permute-start(bf16[256,128]{1,0:T(8,128)(2,1)S(1)} %get-tuple-element.72), channel_id=1, source_target_pairs={{0,2},{1,3},{2,0},{3,1},{4,6},{5,7},{6,4},{7,5},{8,10},{9,11},{10,... | collective-permute-start | bytes 196616 | tf_op jit(solution)/shard_map/ppermute | solution.py:29
  27.4 0.1 shard_map.79
  27.4 0.5 collective-permute-start.16
  27.9 2.6 %collective-permute-start.17 = (bf16[256,256]{1,0:T(8,128)(2,1)S(1)}, bf16[256,256]{1,0:T(8,128)(2,1)S(1)}, u32[]{:S(2)}, u32[]{:S(2)}) collective-permute-start(bf16[256,256]{1,0:T(8,128)(2,1)S(1)} %get-tuple-element.83), channel_id=1, source_target_pairs={{0,4},{1,5},{2,6},{3,7},{4,0},{5,1},{6,2},{7,3},{8,12},{9,13},{10,... | collective-permute-start | bytes 393224 | tf_op jit(solution)/shard_map/ppermute | solution.py:29
  30.5 0.2 collective-permute-done.3.refs_2_
  30.8 3.6 %collective-permute-start.18 = (bf16[256,256]{1,0:T(8,128)(2,1)S(1)}, bf16[256,256]{1,0:T(8,128)(2,1)S(1)}, u32[]{:S(2)}, u32[]{:S(2)}) collective-permute-start(bf16[256,256]{1,0:T(8,128)(2,1)S(1)} %get-tuple-element.84), channel_id=1, source_target_pairs={{0,6},{1,7},{2,4},{3,5},{4,2},{5,3},{6,0},{7,1},{8,14},{9,15},{10,... | collective-permute-start | bytes 393224 | tf_op jit(solution)/shard_map/ppermute | solution.py:29
  34.4 1.9 %collective-permute-start.12 = (bf16[256,128]{1,0:T(8,128)(2,1)S(1)}, bf16[256,128]{1,0:T(8,128)(2,1)S(1)}, u32[]{:S(2)}, u32[]{:S(2)}) collective-permute-start(bf16[256,128]{1,0:T(8,128)(2,1)S(1)} %get-tuple-element.74), channel_id=1, source_target_pairs={{0,6},{1,7},{2,4},{3,5},{4,2},{5,3},{6,0},{7,1},{8,14},{9,15},{10,... | collective-permute-start | bytes 196616 | tf_op jit(solution)/shard_map/ppermute | solution.py:29
  36.3 10.3 %collective-permute-done.11.refs_6_ = bf16[256,128]{1,0:T(8,128)(2,1)S(1)} collective-permute-done((bf16[256,128]{1,0:T(8,128)(2,1)S(1)}, bf16[256,128]{1,0:T(8,128)(2,1)S(1)}, u32[]{:S(2)}, u32[]{:S(2)}) %collective-permute-start.11) | collective-permute-done | bytes 65568 | tf_op jit(solution)/shard_map/ppermute | solution.py:29
  46.6 0.0 collective-permute-done.18.refs_11_
  46.6 0.5 shard_map.80
  47.1 0.1 collective-permute-start.19
  47.2 0.4 shard_map.82
  47.6 1.7 %collective-permute-start.23 = (bf16[256,128]{1,0:T(8,128)(2,1)S(1)}, bf16[256,128]{1,0:T(8,128)(2,1)S(1)}, u32[]{:S(2)}, u32[]{:S(2)}) collective-permute-start(bf16[256,128]{1,0:T(8,128)(2,1)S(1)} %get-tuple-element.92), channel_id=1, source_target_pairs={{0,8},{8,0},{16,24},{24,16},{1,9},{9,1},{17,25},{25,17},{2,10},{10... | collective-permute-start | bytes 196616 | tf_op jit(solution)/shard_map/ppermute | solution.py:29
  49.3 1.0 %collective-permute-start.24 = (bf16[256,128]{1,0:T(8,128)(2,1)S(1)}, bf16[256,128]{1,0:T(8,128)(2,1)S(1)}, u32[]{:S(2)}, u32[]{:S(2)}) collective-permute-start(bf16[256,128]{1,0:T(8,128)(2,1)S(1)} %get-tuple-element.93), channel_id=1, source_target_pairs={{0,16},{8,24},{16,0},{24,8},{1,17},{9,25},{17,1},{25,9},{2,18},{10... | collective-permute-start | bytes 196616 | tf_op jit(solution)/shard_map/ppermute | solution.py:29
  50.3 0.8 %collective-permute-start.25 = (bf16[256,128]{1,0:T(8,128)(2,1)S(1)}, bf16[256,128]{1,0:T(8,128)(2,1)S(1)}, u32[]{:S(2)}, u32[]{:S(2)}) collective-permute-start(bf16[256,128]{1,0:T(8,128)(2,1)S(1)} %get-tuple-element.94), channel_id=1, source_target_pairs={{0,24},{8,16},{16,8},{24,0},{1,25},{9,17},{17,9},{25,1},{2,26},{10... | collective-permute-start | bytes 196616 | tf_op jit(solution)/shard_map/ppermute | solution.py:29
  51.2 1.0 %collective-permute-done.23.refs_1_ = bf16[256,128]{1,0:T(8,128)(2,1)S(1)} collective-permute-done((bf16[256,128]{1,0:T(8,128)(2,1)S(1)}, bf16[256,128]{1,0:T(8,128)(2,1)S(1)}, u32[]{:S(2)}, u32[]{:S(2)}) %collective-permute-start.23) | collective-permute-done | bytes 65568 | tf_op jit(solution)/shard_map/ppermute | solution.py:29
  52.2 1.4 %collective-permute-done.24.refs_2_ = bf16[256,128]{1,0:T(8,128)(2,1)S(1)} collective-permute-done((bf16[256,128]{1,0:T(8,128)(2,1)S(1)}, bf16[256,128]{1,0:T(8,128)(2,1)S(1)}, u32[]{:S(2)}, u32[]{:S(2)}) %collective-permute-start.24) | collective-permute-done | bytes 65568 | tf_op jit(solution)/shard_map/ppermute | solution.py:29
  53.5 1.9 %collective-permute-done.25.refs_3_ = bf16[256,128]{1,0:T(8,128)(2,1)S(1)} collective-permute-done((bf16[256,128]{1,0:T(8,128)(2,1)S(1)}, bf16[256,128]{1,0:T(8,128)(2,1)S(1)}, u32[]{:S(2)}, u32[]{:S(2)}) %collective-permute-start.25) | collective-permute-done | bytes 65568 | tf_op jit(solution)/shard_map/ppermute | solution.py:29
  55.5 1.3 %collective-permute-start.26 = (bf16[256,128]{1,0:T(8,128)(2,1)S(1)}, bf16[256,128]{1,0:T(8,128)(2,1)S(1)}, u32[]{:S(2)}, u32[]{:S(2)}) collective-permute-start(bf16[256,128]{1,0:T(8,128)(2,1)S(1)} %get-tuple-element.96), channel_id=1, source_target_pairs={{0,2},{1,3},{2,0},{3,1},{4,6},{5,7},{6,4},{7,5},{8,10},{9,11},{10,... | collective-permute-start | bytes 196616 | tf_op jit(solution)/shard_map/ppermute | solution.py:29
  56.8 1.7 %collective-permute-start.27 = (bf16[256,128]{1,0:T(8,128)(2,1)S(1)}, bf16[256,128]{1,0:T(8,128)(2,1)S(1)}, u32[]{:S(2)}, u32[]{:S(2)}) collective-permute-start(bf16[256,128]{1,0:T(8,128)(2,1)S(1)} %get-tuple-element.97), channel_id=1, source_target_pairs={{0,4},{1,5},{2,6},{3,7},{4,0},{5,1},{6,2},{7,3},{8,12},{9,13},{10,... | collective-permute-start | bytes 196616 | tf_op jit(solution)/shard_map/ppermute | solution.py:29
  58.5 1.5 %collective-permute-start.28 = (bf16[256,128]{1,0:T(8,128)(2,1)S(1)}, bf16[256,128]{1,0:T(8,128)(2,1)S(1)}, u32[]{:S(2)}, u32[]{:S(2)}) collective-permute-start(bf16[256,128]{1,0:T(8,128)(2,1)S(1)} %get-tuple-element.98), channel_id=1, source_target_pairs={{0,6},{1,7},{2,4},{3,5},{4,2},{5,3},{6,0},{7,1},{8,14},{9,15},{10,... | collective-permute-start | bytes 196616 | tf_op jit(solution)/shard_map/ppermute | solution.py:29
  60.0 0.0 collective-permute-done.26.refs_5_
  60.0 3.3 %collective-permute-done.27.refs_6_ = bf16[256,128]{1,0:T(8,128)(2,1)S(1)} collective-permute-done((bf16[256,128]{1,0:T(8,128)(2,1)S(1)}, bf16[256,128]{1,0:T(8,128)(2,1)S(1)}, u32[]{:S(2)}, u32[]{:S(2)}) %collective-permute-start.27) | collective-permute-done | bytes 65568 | tf_op jit(solution)/shard_map/ppermute | solution.py:29
  63.3 1.4 %collective-permute-done.28.refs_7_ = bf16[256,128]{1,0:T(8,128)(2,1)S(1)} collective-permute-done((bf16[256,128]{1,0:T(8,128)(2,1)S(1)}, bf16[256,128]{1,0:T(8,128)(2,1)S(1)}, u32[]{:S(2)}, u32[]{:S(2)}) %collective-permute-start.28) | collective-permute-done | bytes 65568 | tf_op jit(solution)/shard_map/ppermute | solution.py:29
  64.7 0.3 shard_map.84
  65.0 0.1 collective-permute-start.29
  65.1 0.0 collective-permute-done.19.other_ref
  65.1 0.1 shard_map.81
  65.2 1.3 %collective-permute-start.20 = (bf16[128,384]{1,0:T(8,128)(2,1)S(1)}, bf16[128,384]{1,0:T(8,128)(2,1)S(1)}, u32[]{:S(2)}, u32[]{:S(2)}) collective-permute-start(bf16[128,384]{1,0:T(8,128)(2,1)S(1)} %get-tuple-element.88), channel_id=1, source_target_pairs={{0,8},{8,0},{16,24},{24,16},{1,9},{9,1},{17,25},{25,17},{2,10},{10... | collective-permute-start | bytes 294920 | tf_op jit(solution)/shard_map/ppermute | solution.py:29
  66.5 0.5 collective-permute-start.21
  67.0 1.7 %collective-permute-start.22 = (bf16[128,384]{1,0:T(8,128)(2,1)S(1)}, bf16[128,384]{1,0:T(8,128)(2,1)S(1)}, u32[]{:S(2)}, u32[]{:S(2)}) collective-permute-start(bf16[128,384]{1,0:T(8,128)(2,1)S(1)} %get-tuple-element.90), channel_id=1, source_target_pairs={{0,24},{8,16},{16,8},{24,0},{1,25},{9,17},{17,9},{25,1},{2,26},{10... | collective-permute-start | bytes 294920 | tf_op jit(solution)/shard_map/ppermute | solution.py:29
  68.7 1.3 %collective-permute-start.30 = (bf16[128,128]{1,0:T(8,128)(2,1)S(1)}, bf16[128,128]{1,0:T(8,128)(2,1)S(1)}, u32[]{:S(2)}, u32[]{:S(2)}) collective-permute-start(bf16[128,128]{1,0:T(8,128)(2,1)S(1)} %get-tuple-element.102), channel_id=1, source_target_pairs={{0,8},{8,0},{16,24},{24,16},{1,9},{9,1},{17,25},{25,17},{2,10},{10... | collective-permute-start | bytes 98312 | tf_op jit(solution)/shard_map/ppermute | solution.py:29
  70.1 0.5 collective-permute-start.31
  70.6 2.7 %collective-permute-done.30.refs_5_ = bf16[128,128]{1,0:T(8,128)(2,1)S(1)} collective-permute-done((bf16[128,128]{1,0:T(8,128)(2,1)S(1)}, bf16[128,128]{1,0:T(8,128)(2,1)S(1)}, u32[]{:S(2)}, u32[]{:S(2)}) %collective-permute-start.30) | collective-permute-done | bytes 32800 | tf_op jit(solution)/shard_map/ppermute | solution.py:29
  73.3 1.6 %collective-permute-start.32 = (bf16[128,128]{1,0:T(8,128)(2,1)S(1)}, bf16[128,128]{1,0:T(8,128)(2,1)S(1)}, u32[]{:S(2)}, u32[]{:S(2)}) collective-permute-start(bf16[128,128]{1,0:T(8,128)(2,1)S(1)} %get-tuple-element.104), channel_id=1, source_target_pairs={{0,24},{8,16},{16,8},{24,0},{1,25},{9,17},{17,9},{25,1},{2,26},{10... | collective-permute-start | bytes 98312 | tf_op jit(solution)/shard_map/ppermute | solution.py:29
  74.9 3.2 %collective-permute-done.32.refs_7_ = bf16[128,128]{1,0:T(8,128)(2,1)S(1)} collective-permute-done((bf16[128,128]{1,0:T(8,128)(2,1)S(1)}, bf16[128,128]{1,0:T(8,128)(2,1)S(1)}, u32[]{:S(2)}, u32[]{:S(2)}) %collective-permute-start.32) | collective-permute-done | bytes 32800 | tf_op jit(solution)/shard_map/ppermute | solution.py:29
  78.1 0.0 collective-permute-done.20.refs_1_
  78.1 0.0 collective-permute-done.21.refs_2_
  78.1 0.7 shard_map.86
  (22 shorter events, 0.1 us)
Async XLA Ops:
  0.0 2.4 %collective-permute-start = (bf16[128,2048]{1,0:T(8,128)(2,1)}, bf16[128,2048]{1,0:T(8,128)(2,1)S(1)}, u32[]{:S(2)}, u32[]{:S(2)}) collective-permute-start(bf16[128,2048]{1,0:T(8,128)(2,1)} %refs_0_.1), channel_id=1, source_target_pairs={{0,1},{1,0},{2,3},{3,2},{4,5},{5,4},{6,7},{7,6},{8,9},{9,8},{10,11... | collective-permute-start | bytes 1572872 | tf_op jit(solution)/shard_map/ppermute | solution.py:29
  0.5 1.9 %collective-permute-start.5 = (bf16[128,512]{1,0:T(8,128)(2,1)}, bf16[128,512]{1,0:T(8,128)(2,1)S(1)}, u32[]{:S(2)}, u32[]{:S(2)}) collective-permute-start(bf16[128,512]{1,0:T(8,128)(2,1)} %refs_1_.1), channel_id=1, source_target_pairs={{0,1},{1,0},{2,3},{3,2},{4,5},{5,4},{6,7},{7,6},{8,9},{9,8},{10,11... | collective-permute-start | bytes 393224 | tf_op jit(solution)/shard_map/ppermute | solution.py:29
  4.0 2.0 %collective-permute-start.6 = (bf16[512,512]{1,0:T(8,128)(2,1)S(1)}, bf16[512,512]{1,0:T(8,128)(2,1)S(1)}, u32[]{:S(2)}, u32[]{:S(2)}) collective-permute-start(bf16[512,512]{1,0:T(8,128)(2,1)S(1)} %get-tuple-element.64.own_ref), channel_id=1, source_target_pairs={{0,1},{1,0},{2,3},{3,2},{4,5},{5,4},{6,7},{7,6},{8,9},{9,8},{10,11... | collective-permute-start | bytes 1572872 | tf_op jit(solution)/shard_map/ppermute | solution.py:29
  8.5 9.6 %collective-permute-start.7 = (bf16[256,128]{1,0:T(8,128)(2,1)S(1)}, bf16[256,128]{1,0:T(8,128)(2,1)S(1)}, u32[]{:S(2)}, u32[]{:S(2)}) collective-permute-start(bf16[256,128]{1,0:T(8,128)(2,1)S(1)} %get-tuple-element.68), channel_id=1, source_target_pairs={{0,8},{8,0},{16,24},{24,16},{1,9},{9,1},{17,25},{25,17},{2,10},{10... | collective-permute-start | bytes 196616 | tf_op jit(solution)/shard_map/ppermute | solution.py:29
  11.9 10.8 %collective-permute-start.13 = (bf16[256,256]{1,0:T(8,128)(2,1)S(1)}, bf16[256,256]{1,0:T(8,128)(2,1)S(1)}, u32[]{:S(2)}, u32[]{:S(2)}) collective-permute-start(bf16[256,256]{1,0:T(8,128)(2,1)S(1)} %get-tuple-element.78), channel_id=1, source_target_pairs={{0,8},{8,0},{16,24},{24,16},{1,9},{9,1},{17,25},{25,17},{2,10},{10... | collective-permute-start | bytes 393224 | tf_op jit(solution)/shard_map/ppermute | solution.py:29
  11.9 3.5 %copy-start.2 = (s32[1,128]{1,0:T(1,128)S(1)}, s32[1,128]{1,0:T(1,128)}, u32[]{:S(2)}) copy-start(s32[1,128]{1,0:T(1,128)} %refs_4_.1) | copy-start | bytes 1540
  12.0 7.2 %collective-permute-start.8 = (bf16[256,128]{1,0:T(8,128)(2,1)S(1)}, bf16[256,128]{1,0:T(8,128)(2,1)S(1)}, u32[]{:S(2)}, u32[]{:S(2)}) collective-permute-start(bf16[256,128]{1,0:T(8,128)(2,1)S(1)} %get-tuple-element.69), channel_id=1, source_target_pairs={{0,16},{8,24},{16,0},{24,8},{1,17},{9,25},{17,1},{25,9},{2,18},{10... | collective-permute-start | bytes 196616 | tf_op jit(solution)/shard_map/ppermute | solution.py:29
  14.0 7.1 %collective-permute-start.9 = (bf16[256,128]{1,0:T(8,128)(2,1)S(1)}, bf16[256,128]{1,0:T(8,128)(2,1)S(1)}, u32[]{:S(2)}, u32[]{:S(2)}) collective-permute-start(bf16[256,128]{1,0:T(8,128)(2,1)S(1)} %get-tuple-element.70), channel_id=1, source_target_pairs={{0,24},{8,16},{16,8},{24,0},{1,25},{9,17},{17,9},{25,1},{2,26},{10... | collective-permute-start | bytes 196616 | tf_op jit(solution)/shard_map/ppermute | solution.py:29
  15.4 1.2 %collective-permute-start.1 = (s32[1,128]{1,0:T(1,128)S(1)}, s32[1,128]{1,0:T(1,128)S(1)}, u32[]{:S(2)}, u32[]{:S(2)}) collective-permute-start(s32[1,128]{1,0:T(1,128)S(1)} %copy-done.2), channel_id=1, source_target_pairs={{0,1},{1,0},{2,3},{3,2},{4,5},{5,4},{6,7},{7,6},{8,9},{9,8},{10,11... | collective-permute-start | bytes 1544 | tf_op jit(solution)/shard_map/ppermute | solution.py:29
  16.6 1.6 %copy-start.1 = (s32[4,8]{1,0:T(4,128)S(1)}, s32[4,8]{1,0:T(4,128)}, u32[]{:S(2)}) copy-start(s32[4,8]{1,0:T(4,128)} %new_ref.1) | copy-start | bytes 388
  16.6 1.6 %copy-start = (s32[4,4]{1,0:T(4,128)S(1)}, s32[4,4]{1,0:T(4,128)}, u32[]{:S(2)}) copy-start(s32[4,4]{1,0:T(4,128)} %old_ref.1) | copy-start | bytes 196
  16.6 9.2 %collective-permute-start.14 = (bf16[256,256]{1,0:T(8,128)(2,1)S(1)}, bf16[256,256]{1,0:T(8,128)(2,1)S(1)}, u32[]{:S(2)}, u32[]{:S(2)}) collective-permute-start(bf16[256,256]{1,0:T(8,128)(2,1)S(1)} %get-tuple-element.79), channel_id=1, source_target_pairs={{0,16},{8,24},{16,0},{24,8},{1,17},{9,25},{17,1},{25,9},{2,18},{10... | collective-permute-start | bytes 393224 | tf_op jit(solution)/shard_map/ppermute | solution.py:29
  18.1 9.2 %collective-permute-start.15 = (bf16[256,256]{1,0:T(8,128)(2,1)S(1)}, bf16[256,256]{1,0:T(8,128)(2,1)S(1)}, u32[]{:S(2)}, u32[]{:S(2)}) collective-permute-start(bf16[256,256]{1,0:T(8,128)(2,1)S(1)} %get-tuple-element.80), channel_id=1, source_target_pairs={{0,24},{8,16},{16,8},{24,0},{1,25},{9,17},{17,9},{25,1},{2,26},{10... | collective-permute-start | bytes 393224 | tf_op jit(solution)/shard_map/ppermute | solution.py:29
  19.1 8.8 %collective-permute-start.2 = (bf16[2,128,256]{2,1,0:T(8,128)(2,1)S(1)}, bf16[2,128,256]{2,1,0:T(8,128)(2,1)S(1)}, u32[]{:S(2)}, u32[]{:S(2)}) collective-permute-start(bf16[2,128,256]{2,1,0:T(8,128)(2,1)S(1)} %get-tuple-element.59), channel_id=1, source_target_pairs={{0,8},{8,0},{16,24},{24,16},{1,9},{9,1},{17,25},{25,17},{2,10},{10... | collective-permute-start | bytes 393224 | tf_op jit(solution)/shard_map/ppermute | solution.py:29
  21.1 9.7 %collective-permute-start.3 = (bf16[2,128,256]{2,1,0:T(8,128)(2,1)S(1)}, bf16[2,128,256]{2,1,0:T(8,128)(2,1)S(1)}, u32[]{:S(2)}, u32[]{:S(2)}) collective-permute-start(bf16[2,128,256]{2,1,0:T(8,128)(2,1)S(1)} %get-tuple-element.60), channel_id=1, source_target_pairs={{0,16},{8,24},{16,0},{24,8},{1,17},{9,25},{17,1},{25,9},{2,18},{10... | collective-permute-start | bytes 393224 | tf_op jit(solution)/shard_map/ppermute | solution.py:29
  22.6 11.7 %collective-permute-start.4 = (bf16[2,128,256]{2,1,0:T(8,128)(2,1)S(1)}, bf16[2,128,256]{2,1,0:T(8,128)(2,1)S(1)}, u32[]{:S(2)}, u32[]{:S(2)}) collective-permute-start(bf16[2,128,256]{2,1,0:T(8,128)(2,1)S(1)} %get-tuple-element.61), channel_id=1, source_target_pairs={{0,24},{8,16},{16,8},{24,0},{1,25},{9,17},{17,9},{25,1},{2,26},{10... | collective-permute-start | bytes 393224 | tf_op jit(solution)/shard_map/ppermute | solution.py:29
  25.8 8.6 %collective-permute-start.10 = (bf16[256,128]{1,0:T(8,128)(2,1)S(1)}, bf16[256,128]{1,0:T(8,128)(2,1)S(1)}, u32[]{:S(2)}, u32[]{:S(2)}) collective-permute-start(bf16[256,128]{1,0:T(8,128)(2,1)S(1)} %get-tuple-element.72), channel_id=1, source_target_pairs={{0,2},{1,3},{2,0},{3,1},{4,6},{5,7},{6,4},{7,5},{8,10},{9,11},{10,... | collective-permute-start | bytes 196616 | tf_op jit(solution)/shard_map/ppermute | solution.py:29
  27.4 19.2 %collective-permute-start.16 = (bf16[256,256]{1,0:T(8,128)(2,1)S(1)}, bf16[256,256]{1,0:T(8,128)(2,1)S(1)}, u32[]{:S(2)}, u32[]{:S(2)}) collective-permute-start(bf16[256,256]{1,0:T(8,128)(2,1)S(1)} %get-tuple-element.82), channel_id=1, source_target_pairs={{0,2},{1,3},{2,0},{3,1},{4,6},{5,7},{6,4},{7,5},{8,10},{9,11},{10,... | collective-permute-start | bytes 393224 | tf_op jit(solution)/shard_map/ppermute | solution.py:29
  27.9 18.6 %collective-permute-start.17 = (bf16[256,256]{1,0:T(8,128)(2,1)S(1)}, bf16[256,256]{1,0:T(8,128)(2,1)S(1)}, u32[]{:S(2)}, u32[]{:S(2)}) collective-permute-start(bf16[256,256]{1,0:T(8,128)(2,1)S(1)} %get-tuple-element.83), channel_id=1, source_target_pairs={{0,4},{1,5},{2,6},{3,7},{4,0},{5,1},{6,2},{7,3},{8,12},{9,13},{10,... | collective-permute-start | bytes 393224 | tf_op jit(solution)/shard_map/ppermute | solution.py:29
  30.8 15.8 %collective-permute-start.18 = (bf16[256,256]{1,0:T(8,128)(2,1)S(1)}, bf16[256,256]{1,0:T(8,128)(2,1)S(1)}, u32[]{:S(2)}, u32[]{:S(2)}) collective-permute-start(bf16[256,256]{1,0:T(8,128)(2,1)S(1)} %get-tuple-element.84), channel_id=1, source_target_pairs={{0,6},{1,7},{2,4},{3,5},{4,2},{5,3},{6,0},{7,1},{8,14},{9,15},{10,... | collective-permute-start | bytes 393224 | tf_op jit(solution)/shard_map/ppermute | solution.py:29
  34.4 12.2 %collective-permute-start.11 = (bf16[256,128]{1,0:T(8,128)(2,1)S(1)}, bf16[256,128]{1,0:T(8,128)(2,1)S(1)}, u32[]{:S(2)}, u32[]{:S(2)}) collective-permute-start(bf16[256,128]{1,0:T(8,128)(2,1)S(1)} %get-tuple-element.73), channel_id=1, source_target_pairs={{0,4},{1,5},{2,6},{3,7},{4,0},{5,1},{6,2},{7,3},{8,12},{9,13},{10,... | collective-permute-start | bytes 196616 | tf_op jit(solution)/shard_map/ppermute | solution.py:29
  34.4 12.2 %collective-permute-start.12 = (bf16[256,128]{1,0:T(8,128)(2,1)S(1)}, bf16[256,128]{1,0:T(8,128)(2,1)S(1)}, u32[]{:S(2)}, u32[]{:S(2)}) collective-permute-start(bf16[256,128]{1,0:T(8,128)(2,1)S(1)} %get-tuple-element.74), channel_id=1, source_target_pairs={{0,6},{1,7},{2,4},{3,5},{4,2},{5,3},{6,0},{7,1},{8,14},{9,15},{10,... | collective-permute-start | bytes 196616 | tf_op jit(solution)/shard_map/ppermute | solution.py:29
  47.1 18.0 %collective-permute-start.19 = (bf16[4,128,384]{2,1,0:T(8,128)(2,1)S(1)}, bf16[4,128,384]{2,1,0:T(8,128)(2,1)S(1)}, u32[]{:S(2)}, u32[]{:S(2)}) collective-permute-start(bf16[4,128,384]{2,1,0:T(8,128)(2,1)S(1)} %get-tuple-element.86), channel_id=1, source_target_pairs={{0,1},{1,0},{2,3},{3,2},{4,5},{5,4},{6,7},{7,6},{8,9},{9,8},{10,11... | collective-permute-start | bytes 1179656 | tf_op jit(solution)/shard_map/ppermute | solution.py:29
  47.6 4.6 %collective-permute-start.23 = (bf16[256,128]{1,0:T(8,128)(2,1)S(1)}, bf16[256,128]{1,0:T(8,128)(2,1)S(1)}, u32[]{:S(2)}, u32[]{:S(2)}) collective-permute-start(bf16[256,128]{1,0:T(8,128)(2,1)S(1)} %get-tuple-element.92), channel_id=1, source_target_pairs={{0,8},{8,0},{16,24},{24,16},{1,9},{9,1},{17,25},{25,17},{2,10},{10... | collective-permute-start | bytes 196616 | tf_op jit(solution)/shard_map/ppermute | solution.py:29
  49.3 4.3 %collective-permute-start.24 = (bf16[256,128]{1,0:T(8,128)(2,1)S(1)}, bf16[256,128]{1,0:T(8,128)(2,1)S(1)}, u32[]{:S(2)}, u32[]{:S(2)}) collective-permute-start(bf16[256,128]{1,0:T(8,128)(2,1)S(1)} %get-tuple-element.93), channel_id=1, source_target_pairs={{0,16},{8,24},{16,0},{24,8},{1,17},{9,25},{17,1},{25,9},{2,18},{10... | collective-permute-start | bytes 196616 | tf_op jit(solution)/shard_map/ppermute | solution.py:29
  50.3 5.2 %collective-permute-start.25 = (bf16[256,128]{1,0:T(8,128)(2,1)S(1)}, bf16[256,128]{1,0:T(8,128)(2,1)S(1)}, u32[]{:S(2)}, u32[]{:S(2)}) collective-permute-start(bf16[256,128]{1,0:T(8,128)(2,1)S(1)} %get-tuple-element.94), channel_id=1, source_target_pairs={{0,24},{8,16},{16,8},{24,0},{1,25},{9,17},{17,9},{25,1},{2,26},{10... | collective-permute-start | bytes 196616 | tf_op jit(solution)/shard_map/ppermute | solution.py:29
  55.5 4.5 %collective-permute-start.26 = (bf16[256,128]{1,0:T(8,128)(2,1)S(1)}, bf16[256,128]{1,0:T(8,128)(2,1)S(1)}, u32[]{:S(2)}, u32[]{:S(2)}) collective-permute-start(bf16[256,128]{1,0:T(8,128)(2,1)S(1)} %get-tuple-element.96), channel_id=1, source_target_pairs={{0,2},{1,3},{2,0},{3,1},{4,6},{5,7},{6,4},{7,5},{8,10},{9,11},{10,... | collective-permute-start | bytes 196616 | tf_op jit(solution)/shard_map/ppermute | solution.py:29
  56.8 6.4 %collective-permute-start.27 = (bf16[256,128]{1,0:T(8,128)(2,1)S(1)}, bf16[256,128]{1,0:T(8,128)(2,1)S(1)}, u32[]{:S(2)}, u32[]{:S(2)}) collective-permute-start(bf16[256,128]{1,0:T(8,128)(2,1)S(1)} %get-tuple-element.97), channel_id=1, source_target_pairs={{0,4},{1,5},{2,6},{3,7},{4,0},{5,1},{6,2},{7,3},{8,12},{9,13},{10,... | collective-permute-start | bytes 196616 | tf_op jit(solution)/shard_map/ppermute | solution.py:29
  58.5 6.2 %collective-permute-start.28 = (bf16[256,128]{1,0:T(8,128)(2,1)S(1)}, bf16[256,128]{1,0:T(8,128)(2,1)S(1)}, u32[]{:S(2)}, u32[]{:S(2)}) collective-permute-start(bf16[256,128]{1,0:T(8,128)(2,1)S(1)} %get-tuple-element.98), channel_id=1, source_target_pairs={{0,6},{1,7},{2,4},{3,5},{4,2},{5,3},{6,0},{7,1},{8,14},{9,15},{10,... | collective-permute-start | bytes 196616 | tf_op jit(solution)/shard_map/ppermute | solution.py:29
  65.0 3.7 %collective-permute-start.29 = (bf16[4,128,128]{2,1,0:T(8,128)(2,1)S(1)}, bf16[4,128,128]{2,1,0:T(8,128)(2,1)S(1)}, u32[]{:S(2)}, u32[]{:S(2)}) collective-permute-start(bf16[4,128,128]{2,1,0:T(8,128)(2,1)S(1)} %get-tuple-element.100), channel_id=1, source_target_pairs={{0,1},{1,0},{2,3},{3,2},{4,5},{5,4},{6,7},{7,6},{8,9},{9,8},{10,11... | collective-permute-start | bytes 393224 | tf_op jit(solution)/shard_map/ppermute | solution.py:29
  65.2 12.9 %collective-permute-start.20 = (bf16[128,384]{1,0:T(8,128)(2,1)S(1)}, bf16[128,384]{1,0:T(8,128)(2,1)S(1)}, u32[]{:S(2)}, u32[]{:S(2)}) collective-permute-start(bf16[128,384]{1,0:T(8,128)(2,1)S(1)} %get-tuple-element.88), channel_id=1, source_target_pairs={{0,8},{8,0},{16,24},{24,16},{1,9},{9,1},{17,25},{25,17},{2,10},{10... | collective-permute-start | bytes 294920 | tf_op jit(solution)/shard_map/ppermute | solution.py:29
  66.5 11.6 %collective-permute-start.21 = (bf16[128,384]{1,0:T(8,128)(2,1)S(1)}, bf16[128,384]{1,0:T(8,128)(2,1)S(1)}, u32[]{:S(2)}, u32[]{:S(2)}) collective-permute-start(bf16[128,384]{1,0:T(8,128)(2,1)S(1)} %get-tuple-element.89), channel_id=1, source_target_pairs={{0,16},{8,24},{16,0},{24,8},{1,17},{9,25},{17,1},{25,9},{2,18},{10... | collective-permute-start | bytes 294920 | tf_op jit(solution)/shard_map/ppermute | solution.py:29
  67.0 11.1 %collective-permute-start.22 = (bf16[128,384]{1,0:T(8,128)(2,1)S(1)}, bf16[128,384]{1,0:T(8,128)(2,1)S(1)}, u32[]{:S(2)}, u32[]{:S(2)}) collective-permute-start(bf16[128,384]{1,0:T(8,128)(2,1)S(1)} %get-tuple-element.90), channel_id=1, source_target_pairs={{0,24},{8,16},{16,8},{24,0},{1,25},{9,17},{17,9},{25,1},{2,26},{10... | collective-permute-start | bytes 294920 | tf_op jit(solution)/shard_map/ppermute | solution.py:29
  68.7 4.5 %collective-permute-start.30 = (bf16[128,128]{1,0:T(8,128)(2,1)S(1)}, bf16[128,128]{1,0:T(8,128)(2,1)S(1)}, u32[]{:S(2)}, u32[]{:S(2)}) collective-permute-start(bf16[128,128]{1,0:T(8,128)(2,1)S(1)} %get-tuple-element.102), channel_id=1, source_target_pairs={{0,8},{8,0},{16,24},{24,16},{1,9},{9,1},{17,25},{25,17},{2,10},{10... | collective-permute-start | bytes 98312 | tf_op jit(solution)/shard_map/ppermute | solution.py:29
  70.1 4.8 %collective-permute-start.31 = (bf16[128,128]{1,0:T(8,128)(2,1)S(1)}, bf16[128,128]{1,0:T(8,128)(2,1)S(1)}, u32[]{:S(2)}, u32[]{:S(2)}) collective-permute-start(bf16[128,128]{1,0:T(8,128)(2,1)S(1)} %get-tuple-element.103), channel_id=1, source_target_pairs={{0,16},{8,24},{16,0},{24,8},{1,17},{9,25},{17,1},{25,9},{2,18},{10... | collective-permute-start | bytes 98312 | tf_op jit(solution)/shard_map/ppermute | solution.py:29
  73.3 4.8 %collective-permute-start.32 = (bf16[128,128]{1,0:T(8,128)(2,1)S(1)}, bf16[128,128]{1,0:T(8,128)(2,1)S(1)}, u32[]{:S(2)}, u32[]{:S(2)}) collective-permute-start(bf16[128,128]{1,0:T(8,128)(2,1)S(1)} %get-tuple-element.104), channel_id=1, source_target_pairs={{0,24},{8,16},{16,8},{24,0},{1,25},{9,17},{17,9},{25,1},{2,26},{10... | collective-permute-start | bytes 98312 | tf_op jit(solution)/shard_map/ppermute | solution.py:29

commit v2 on v1

--- a/solution.py
+++ b/solution.py
@@ -16,8 +16,8 @@
 step_scale = 0.01
 gram_eps = 1e-06
 contract_rows = (((0,), (0,)), ((), ()))
-WIDTHS = (1, 2, 1)
-TAILS = ((0, 1), (2,))
+WIDTHS = (1, 1)
+TAILS = ((0,), (1,))
 MOST_PERMUTES = 4
 LANES = 128
 bf16 = jnp.bfloat16
@@ -301,21 +301,25 @@
 
     peer_tokens = swapped(tokens)
     peer_cot = swapped(cotangent)
-    peer_ids = swapped(row_ids)
-    to_load = [tokens, cotangent, momentum, weight, row_ids]
-    tokens_in, cot_in, momentum_in, weight_in, ids_in = call(
-        functools.partial(load_kernel, len(to_load)),
-        to_load,
-        [(a.shape, a.dtype) for a in to_load],
-        [pltpu.SemaphoreType.DMA((len(to_load),))],
-        spaces=[HBM] * len(to_load),
-    )
+
+    def loaded(*arrays):
+        return call(
+            functools.partial(load_kernel, len(arrays)),
+            arrays,
+            [(a.shape, a.dtype) for a in arrays],
+            [pltpu.SemaphoreType.DMA((len(arrays),))],
+            spaces=[HBM] * len(arrays),
+        )
+
+    tokens_in, cot_in, momentum_in = loaded(tokens, cotangent, momentum)
     x0, own_gram = call(
         front_kernel,
         [tokens_in, peer_tokens, cot_in, peer_cot, momentum_in],
         [((half_rows, hidden), bf16), ((hidden, hidden), bf16)],
     )
     peer_gram = swapped(own_gram)
+    weight_in, ids_in = loaded(weight, row_ids)
+    peer_ids = swapped(row_ids)
 
     which, *token_cuts = call(
         functools.partial(choose_kernel, hosts),

time: 79 us -> 63.2 us (0.80)
  waiting for transfers between devices: 31.3 us -> 20.4 us
  starting transfers between devices: 37.9 us -> 32.7 us
    ppermute x33 -> x27, waiting for transfers between devices: 31.3 us -> 20.4 us  [shifted(): return lax.ppermute(shard, axis, [(i, i ^ k * stride) for i in range(size)])]
    ppermute x33 -> x27, starting transfers between devices: 37.9 us -> 32.7 us  [shifted(): return lax.ppermute(shard, axis, [(i, i ^ k * stride) for i in range(size)])]
    pallas_call x14 -> x13, Pallas kernels: 9.45 us -> 9.86 us  [call(): pl.pallas_call(kernel, out_shape=[made[where](*out) for where, out in zip...]
  transfers between devices with their start and end apart: 33 -> 27, of which waited for: 13 -> 13; matrix products, arithmetic and copies ran while one was open for 0% -> 0% of each run, Pallas kernels for 5% -> 7%
where the time goes in v2:
time: 63.2 us; the launch traced here: 63.1 us
  starting transfers between devices  32.7 us (52%)
  waiting for transfers between devices  20.4 us (32%)
  Pallas kernels  9.86 us (16%)
    ppermute x27, starting transfers between devices, shifted(): return lax.ppermute(shard, axis, [(i, i ^ k * stride) for i in range(size)])  32.7 us
    ppermute x27, waiting for transfers between devices, shifted(): return lax.ppermute(shard, axis, [(i, i ^ k * stride) for i in range(size)])  20.4 us
    pallas_call x13, Pallas kernels, call(): pl.pallas_call(kernel, out_shape=[made[where](*out) for where, out in zip...  9.86 us
  transfers between devices with their start and end apart: 27, of which 13 were waited for; matrix products, arithmetic and copies ran while one was open for 0% of the time, Pallas kernels for 7%

profile of v2, /device:TPU:0, one launch (start us, length us, event | category | flops | bytes accessed | tf_op | source)
XLA Modules:
  0.0 63.1 jit_solution(1266519859915292946)
XLA Ops:
  0.0 0.5 collective-permute-start
  0.5 0.0 collective-permute-start.5
  0.5 1.5 %shard_map.73 = (bf16[128,2048]{1,0:T(8,128)(2,1)S(1)}, bf16[128,512]{1,0:T(8,128)(2,1)S(1)}, bf16[1024,512]{1,0:T(8,128)(2,1)S(1)}) custom-call(bf16[128,2048]{1,0:T(8,128)(2,1)} %refs_0_.1, bf16[128,512]{1,0:T(8,128)(2,1)} %refs_1_.2, bf16[1024,512]{1,0:T(8,128)(2,1)} %bitcast.3), custom_call_target="tpu_custom_call" | custom-call | tf_op jit(solution)/shard_map/pallas_call | solution.py:245
  2.0 0.5 collective-permute-done.5.peer_cot_ref
  2.4 0.0 collective-permute-done.peer_ref
  2.4 1.5 %shard_map.76 = (bf16[1024,512]{1,0:T(8,128)(2,1)S(1)}, bf16[512,512]{1,0:T(8,128)(2,1)S(1)}) custom-call(bf16[128,2048]{1,0:T(8,128)(2,1)S(1)} %get-tuple-element.47.own_ref, bf16[128,2048]{1,0:T(8,128)(2,1)S(1)} %collective-permute-done.peer_ref, bf16[128,512]{1,0:T(8,128)(2,1)S(1)} %get-tuple-element.54.cot_ref, ...), custom_call_target="tpu_custom_call" | custom-call | tf_op jit(solution)/shard_map/pallas_call | solution.py:245
  4.0 0.4 collective-permute-start.6
  4.4 1.2 %shard_map.74 = (bf16[1024,512]{1,0:T(8,128)(2,1)S(1)}, s32[1,128]{1,0:T(1,128)S(1)}) custom-call(bf16[1024,512]{1,0:T(8,128)(2,1)} %bitcast.2, s32[1,128]{1,0:T(1,128)} %refs_1_.3), custom_call_target="tpu_custom_call" | custom-call | tf_op jit(solution)/shard_map/pallas_call | solution.py:245
  5.7 0.3 collective-permute-done.6.peer_ref
  6.0 2.5 %shard_map.77 = (bf16[512,512]{1,0:T(8,128)(2,1)S(1)}, f32[8,128]{1,0:T(8,128)S(1)}, bf16[256,256]{1,0:T(8,128)(2,1)S(1)}, bf16[256,256]{1,0:T(8,128)(2,1)S(1)},...) custom-call(bf16[512,512]{1,0:T(8,128)(2,1)S(1)} %get-tuple-element.56.own_ref, ...), custom_call_target="tpu_custom_call" | custom-call | tf_op jit(solution)/shard_map/pallas_call | solution.py:245
  8.5 0.5 shard_map.81
  9.0 0.0 copy-start.2
  9.0 2.9 %collective-permute-start.17 = (bf16[256,256]{1,0:T(8,128)(2,1)S(1)}, bf16[256,256]{1,0:T(8,128)(2,1)S(1)}, u32[]{:S(2)}, u32[]{:S(2)}) collective-permute-start(bf16[256,256]{1,0:T(8,128)(2,1)S(1)} %get-tuple-element.76), channel_id=1, source_target_pairs={{0,8},{8,0},{16,24},{24,16},{1,9},{9,1},{17,25},{25,17},{2,10},{10... | collective-permute-start | bytes 393224 | tf_op jit(solution)/shard_map/ppermute | solution.py:29
  11.9 1.5 %collective-permute-start.18 = (bf16[256,256]{1,0:T(8,128)(2,1)S(1)}, bf16[256,256]{1,0:T(8,128)(2,1)S(1)}, u32[]{:S(2)}, u32[]{:S(2)}) collective-permute-start(bf16[256,256]{1,0:T(8,128)(2,1)S(1)} %get-tuple-element.77), channel_id=1, source_target_pairs={{0,16},{8,24},{16,0},{24,8},{1,17},{9,25},{17,1},{25,9},{2,18},{10... | collective-permute-start | bytes 393224 | tf_op jit(solution)/shard_map/ppermute | solution.py:29
  13.5 0.0 collective-permute-start.1
  13.5 0.1 collective-permute-start.19
  13.6 1.0 %collective-permute-done.1.peer_ids_ref = s32[1,128]{1,0:T(1,128)S(1)} collective-permute-done((s32[1,128]{1,0:T(1,128)S(1)}, s32[1,128]{1,0:T(1,128)S(1)}, u32[]{:S(2)}, u32[]{:S(2)}) %collective-permute-start.1) | collective-permute-done | bytes 544 | tf_op jit(solution)/shard_map/ppermute | solution.py:29
  14.6 0.9 %shard_map.75 = (s32[8]{0:T(128)S(4)}, bf16[2,128,256]{2,1,0:T(8,128)(2,1)S(1)}, bf16[2,128,256]{2,1,0:T(8,128)(2,1)S(1)}, bf16[2,128,256]{2,1,0:T(8,128)(2,1)S(1)}, bf16[2,128,256]{2,1,0:T(8,128)(2,1)S(1)}) custom-call(s32[4,4]{1,0:T(4,128)S(1)} %copy-done, s32[4,8]{1,0:T(4,128)S(1)} %copy-done.1, bf16[128,2048]{1,0:T(8,128)(2,1)S(1)} %get-tuple-element.47.own_ref, ...), custom_call_target="tpu_custom_call" | custom-call | tf_op jit(solution)/shard_map/pallas_call | solution.py:245
  15.6 0.9 %collective-permute-start.2 = (bf16[2,128,256]{2,1,0:T(8,128)(2,1)S(1)}, bf16[2,128,256]{2,1,0:T(8,128)(2,1)S(1)}, u32[]{:S(2)}, u32[]{:S(2)}) collective-permute-start(bf16[2,128,256]{2,1,0:T(8,128)(2,1)S(1)} %get-tuple-element.51), channel_id=1, source_target_pairs={{0,8},{8,0},{16,24},{24,16},{1,9},{9,1},{17,25},{25,17},{2,10},{10... | collective-permute-start | bytes 393224 | tf_op jit(solution)/shard_map/ppermute | solution.py:29
  16.5 1.2 %collective-permute-start.7 = (bf16[256,256]{1,0:T(8,128)(2,1)S(1)}, bf16[256,256]{1,0:T(8,128)(2,1)S(1)}, u32[]{:S(2)}, u32[]{:S(2)}) collective-permute-start(bf16[256,256]{1,0:T(8,128)(2,1)S(1)} %get-tuple-element.60), channel_id=1, source_target_pairs={{0,8},{8,0},{16,24},{24,16},{1,9},{9,1},{17,25},{25,17},{2,10},{10... | collective-permute-start | bytes 393224 | tf_op jit(solution)/shard_map/ppermute | solution.py:29
  17.7 0.0 collective-permute-done.17.refs_1_
  17.7 0.9 %collective-permute-start.8 = (bf16[256,256]{1,0:T(8,128)(2,1)S(1)}, bf16[256,256]{1,0:T(8,128)(2,1)S(1)}, u32[]{:S(2)}, u32[]{:S(2)}) collective-permute-start(bf16[256,256]{1,0:T(8,128)(2,1)S(1)} %get-tuple-element.61), channel_id=1, source_target_pairs={{0,16},{8,24},{16,0},{24,8},{1,17},{9,25},{17,1},{25,9},{2,18},{10... | collective-permute-start | bytes 393224 | tf_op jit(solution)/shard_map/ppermute | solution.py:29
  18.5 0.9 %collective-permute-done.18.refs_2_ = bf16[256,256]{1,0:T(8,128)(2,1)S(1)} collective-permute-done((bf16[256,256]{1,0:T(8,128)(2,1)S(1)}, bf16[256,256]{1,0:T(8,128)(2,1)S(1)}, u32[]{:S(2)}, u32[]{:S(2)}) %collective-permute-start.18) | collective-permute-done | bytes 131104 | tf_op jit(solution)/shard_map/ppermute | solution.py:29
  19.4 1.7 %collective-permute-start.9 = (bf16[256,256]{1,0:T(8,128)(2,1)S(1)}, bf16[256,256]{1,0:T(8,128)(2,1)S(1)}, u32[]{:S(2)}, u32[]{:S(2)}) collective-permute-start(bf16[256,256]{1,0:T(8,128)(2,1)S(1)} %get-tuple-element.62), channel_id=1, source_target_pairs={{0,24},{8,16},{16,8},{24,0},{1,25},{9,17},{17,9},{25,1},{2,26},{10... | collective-permute-start | bytes 393224 | tf_op jit(solution)/shard_map/ppermute | solution.py:29
  21.1 0.0 collective-permute-done.19.refs_3_
  21.1 0.9 %collective-permute-start.3 = (bf16[2,128,256]{2,1,0:T(8,128)(2,1)S(1)}, bf16[2,128,256]{2,1,0:T(8,128)(2,1)S(1)}, u32[]{:S(2)}, u32[]{:S(2)}) collective-permute-start(bf16[2,128,256]{2,1,0:T(8,128)(2,1)S(1)} %get-tuple-element.52), channel_id=1, source_target_pairs={{0,16},{8,24},{16,0},{24,8},{1,17},{9,25},{17,1},{25,9},{2,18},{10... | collective-permute-start | bytes 393224 | tf_op jit(solution)/shard_map/ppermute | solution.py:29
  22.0 0.1 shard_map.82
  22.1 0.5 collective-permute-done.2.refs_1_
  22.6 2.5 %collective-permute-start.4 = (bf16[2,128,256]{2,1,0:T(8,128)(2,1)S(1)}, bf16[2,128,256]{2,1,0:T(8,128)(2,1)S(1)}, u32[]{:S(2)}, u32[]{:S(2)}) collective-permute-start(bf16[2,128,256]{2,1,0:T(8,128)(2,1)S(1)} %get-tuple-element.53), channel_id=1, source_target_pairs={{0,24},{8,16},{16,8},{24,0},{1,25},{9,17},{17,9},{25,1},{2,26},{10... | collective-permute-start | bytes 393224 | tf_op jit(solution)/shard_map/ppermute | solution.py:29
  25.1 0.4 collective-permute-done.7.refs_1_
  25.4 1.6 %collective-permute-start.20 = (bf16[256,256]{1,0:T(8,128)(2,1)S(1)}, bf16[256,256]{1,0:T(8,128)(2,1)S(1)}, u32[]{:S(2)}, u32[]{:S(2)}) collective-permute-start(bf16[256,256]{1,0:T(8,128)(2,1)S(1)} %get-tuple-element.80), channel_id=1, source_target_pairs={{0,2},{1,3},{2,0},{3,1},{4,6},{5,7},{6,4},{7,5},{8,10},{9,11},{10,... | collective-permute-start | bytes 393224 | tf_op jit(solution)/shard_map/ppermute | solution.py:29
  27.0 0.0 collective-permute-done.8.refs_2_
  27.0 2.6 %collective-permute-start.21 = (bf16[256,256]{1,0:T(8,128)(2,1)S(1)}, bf16[256,256]{1,0:T(8,128)(2,1)S(1)}, u32[]{:S(2)}, u32[]{:S(2)}) collective-permute-start(bf16[256,256]{1,0:T(8,128)(2,1)S(1)} %get-tuple-element.81), channel_id=1, source_target_pairs={{0,4},{1,5},{2,6},{3,7},{4,0},{5,1},{6,2},{7,3},{8,12},{9,13},{10,... | collective-permute-start | bytes 393224 | tf_op jit(solution)/shard_map/ppermute | solution.py:29
  29.6 0.0 collective-permute-done.9.refs_3_
  29.6 3.2 %collective-permute-start.22 = (bf16[256,256]{1,0:T(8,128)(2,1)S(1)}, bf16[256,256]{1,0:T(8,128)(2,1)S(1)}, u32[]{:S(2)}, u32[]{:S(2)}) collective-permute-start(bf16[256,256]{1,0:T(8,128)(2,1)S(1)} %get-tuple-element.82), channel_id=1, source_target_pairs={{0,6},{1,7},{2,4},{3,5},{4,2},{5,3},{6,0},{7,1},{8,14},{9,15},{10,... | collective-permute-start | bytes 393224 | tf_op jit(solution)/shard_map/ppermute | solution.py:29
  32.9 0.1 shard_map.78
  32.9 0.0 collective-permute-done.3.refs_2_
  32.9 0.6 collective-permute-start.10
  33.5 0.0 collective-permute-done.4.refs_3_
  33.5 2.6 %collective-permute-start.11 = (bf16[256,256]{1,0:T(8,128)(2,1)S(1)}, bf16[256,256]{1,0:T(8,128)(2,1)S(1)}, u32[]{:S(2)}, u32[]{:S(2)}) collective-permute-start(bf16[256,256]{1,0:T(8,128)(2,1)S(1)} %get-tuple-element.65), channel_id=1, source_target_pairs={{0,4},{1,5},{2,6},{3,7},{4,0},{5,1},{6,2},{7,3},{8,12},{9,13},{10,... | collective-permute-start | bytes 393224 | tf_op jit(solution)/shard_map/ppermute | solution.py:29
  36.1 0.0 collective-permute-done.20.refs_5_
  36.1 1.3 %collective-permute-start.12 = (bf16[256,256]{1,0:T(8,128)(2,1)S(1)}, bf16[256,256]{1,0:T(8,128)(2,1)S(1)}, u32[]{:S(2)}, u32[]{:S(2)}) collective-permute-start(bf16[256,256]{1,0:T(8,128)(2,1)S(1)} %get-tuple-element.66), channel_id=1, source_target_pairs={{0,6},{1,7},{2,4},{3,5},{4,2},{5,3},{6,0},{7,1},{8,14},{9,15},{10,... | collective-permute-start | bytes 393224 | tf_op jit(solution)/shard_map/ppermute | solution.py:29
  37.4 1.2 %collective-permute-done.21.refs_6_ = bf16[256,256]{1,0:T(8,128)(2,1)S(1)} collective-permute-done((bf16[256,256]{1,0:T(8,128)(2,1)S(1)}, bf16[256,256]{1,0:T(8,128)(2,1)S(1)}, u32[]{:S(2)}, u32[]{:S(2)}) %collective-permute-start.21) | collective-permute-done | bytes 131104 | tf_op jit(solution)/shard_map/ppermute | solution.py:29
  38.6 0.8 %collective-permute-done.22.refs_7_ = bf16[256,256]{1,0:T(8,128)(2,1)S(1)} collective-permute-done((bf16[256,256]{1,0:T(8,128)(2,1)S(1)}, bf16[256,256]{1,0:T(8,128)(2,1)S(1)}, u32[]{:S(2)}, u32[]{:S(2)}) %collective-permute-start.22) | collective-permute-done | bytes 131104 | tf_op jit(solution)/shard_map/ppermute | solution.py:29
  39.5 0.3 shard_map.83
  39.8 0.1 collective-permute-start.23
  39.9 0.2 collective-permute-done.10.refs_5_
  40.1 10.2 %collective-permute-done.11.refs_6_ = bf16[256,256]{1,0:T(8,128)(2,1)S(1)} collective-permute-done((bf16[256,256]{1,0:T(8,128)(2,1)S(1)}, bf16[256,256]{1,0:T(8,128)(2,1)S(1)}, u32[]{:S(2)}, u32[]{:S(2)}) %collective-permute-start.11) | collective-permute-done | bytes 131104 | tf_op jit(solution)/shard_map/ppermute | solution.py:29
  50.3 0.0 collective-permute-done.12.refs_7_
  50.3 0.3 shard_map.79
  50.6 0.1 collective-permute-start.13
  50.7 0.0 collective-permute-done.23.other_ref
  50.8 1.0 %collective-permute-start.24 = (bf16[128,256]{1,0:T(8,128)(2,1)S(1)}, bf16[128,256]{1,0:T(8,128)(2,1)S(1)}, u32[]{:S(2)}, u32[]{:S(2)}) collective-permute-start(bf16[128,256]{1,0:T(8,128)(2,1)S(1)} %get-tuple-element.86), channel_id=1, source_target_pairs={{0,8},{8,0},{16,24},{24,16},{1,9},{9,1},{17,25},{25,17},{2,10},{10... | collective-permute-start | bytes 196616 | tf_op jit(solution)/shard_map/ppermute | solution.py:29
  51.8 1.7 %collective-permute-start.25 = (bf16[128,256]{1,0:T(8,128)(2,1)S(1)}, bf16[128,256]{1,0:T(8,128)(2,1)S(1)}, u32[]{:S(2)}, u32[]{:S(2)}) collective-permute-start(bf16[128,256]{1,0:T(8,128)(2,1)S(1)} %get-tuple-element.87), channel_id=1, source_target_pairs={{0,16},{8,24},{16,0},{24,8},{1,17},{9,25},{17,1},{25,9},{2,18},{10... | collective-permute-start | bytes 196616 | tf_op jit(solution)/shard_map/ppermute | solution.py:29
  53.6 0.8 %collective-permute-start.26 = (bf16[128,256]{1,0:T(8,128)(2,1)S(1)}, bf16[128,256]{1,0:T(8,128)(2,1)S(1)}, u32[]{:S(2)}, u32[]{:S(2)}) collective-permute-start(bf16[128,256]{1,0:T(8,128)(2,1)S(1)} %get-tuple-element.88), channel_id=1, source_target_pairs={{0,24},{8,16},{16,8},{24,0},{1,25},{9,17},{17,9},{25,1},{2,26},{10... | collective-permute-start | bytes 196616 | tf_op jit(solution)/shard_map/ppermute | solution.py:29
  54.3 0.0 collective-permute-done.13.other_ref
  54.4 1.0 %collective-permute-start.14 = (bf16[128,256]{1,0:T(8,128)(2,1)S(1)}, bf16[128,256]{1,0:T(8,128)(2,1)S(1)}, u32[]{:S(2)}, u32[]{:S(2)}) collective-permute-start(bf16[128,256]{1,0:T(8,128)(2,1)S(1)} %get-tuple-element.70), channel_id=1, source_target_pairs={{0,8},{8,0},{16,24},{24,16},{1,9},{9,1},{17,25},{25,17},{2,10},{10... | collective-permute-start | bytes 196616 | tf_op jit(solution)/shard_map/ppermute | solution.py:29
  55.4 1.7 %collective-permute-start.15 = (bf16[128,256]{1,0:T(8,128)(2,1)S(1)}, bf16[128,256]{1,0:T(8,128)(2,1)S(1)}, u32[]{:S(2)}, u32[]{:S(2)}) collective-permute-start(bf16[128,256]{1,0:T(8,128)(2,1)S(1)} %get-tuple-element.71), channel_id=1, source_target_pairs={{0,16},{8,24},{16,0},{24,8},{1,17},{9,25},{17,1},{25,9},{2,18},{10... | collective-permute-start | bytes 196616 | tf_op jit(solution)/shard_map/ppermute | solution.py:29
  57.2 0.0 collective-permute-done.24.refs_5_
  57.2 0.8 %collective-permute-start.16 = (bf16[128,256]{1,0:T(8,128)(2,1)S(1)}, bf16[128,256]{1,0:T(8,128)(2,1)S(1)}, u32[]{:S(2)}, u32[]{:S(2)}) collective-permute-start(bf16[128,256]{1,0:T(8,128)(2,1)S(1)} %get-tuple-element.72), channel_id=1, source_target_pairs={{0,24},{8,16},{16,8},{24,0},{1,25},{9,17},{17,9},{25,1},{2,26},{10... | collective-permute-start | bytes 196616 | tf_op jit(solution)/shard_map/ppermute | solution.py:29
  58.0 1.3 %collective-permute-done.26.refs_7_ = bf16[128,256]{1,0:T(8,128)(2,1)S(1)} collective-permute-done((bf16[128,256]{1,0:T(8,128)(2,1)S(1)}, bf16[128,256]{1,0:T(8,128)(2,1)S(1)}, u32[]{:S(2)}, u32[]{:S(2)}) %collective-permute-start.26) | collective-permute-done | bytes 65568 | tf_op jit(solution)/shard_map/ppermute | solution.py:29
  59.3 0.8 %collective-permute-done.15.refs_2_ = bf16[128,256]{1,0:T(8,128)(2,1)S(1)} collective-permute-done((bf16[128,256]{1,0:T(8,128)(2,1)S(1)}, bf16[128,256]{1,0:T(8,128)(2,1)S(1)}, u32[]{:S(2)}, u32[]{:S(2)}) %collective-permute-start.15) | collective-permute-done | bytes 65568 | tf_op jit(solution)/shard_map/ppermute | solution.py:29
  60.1 2.3 %collective-permute-done.16.refs_3_ = bf16[128,256]{1,0:T(8,128)(2,1)S(1)} collective-permute-done((bf16[128,256]{1,0:T(8,128)(2,1)S(1)}, bf16[128,256]{1,0:T(8,128)(2,1)S(1)}, u32[]{:S(2)}, u32[]{:S(2)}) %collective-permute-start.16) | collective-permute-done | bytes 65568 | tf_op jit(solution)/shard_map/ppermute | solution.py:29
  62.3 0.7 %shard_map.85 = bf16[128,512]{1,0:T(8,128)(2,1)} custom-call(bf16[128,256]{1,0:T(8,128)(2,1)S(1)} %get-tuple-element.69.refs_0_, bf16[128,256]{1,0:T(8,128)(2,1)S(1)} %collective-permute-done.14.refs_1_, bf16[128,256]{1,0:T(8,128)(2,1)S(1)} %collective-permute-done.15.refs_2_, bf16[128,256]{1,0:T(8,128)(2,1)S(1)} %collective-permute-done.16.refs_3_, ...), custom_call_target="tpu_custom_call" | custom-call | tf_op jit(solution)/shard_map/pallas_call | solution.py:245
  (9 shorter events, 0.1 us)
Async XLA Ops:
  0.0 2.4 %collective-permute-start = (bf16[128,2048]{1,0:T(8,128)(2,1)}, bf16[128,2048]{1,0:T(8,128)(2,1)S(1)}, u32[]{:S(2)}, u32[]{:S(2)}) collective-permute-start(bf16[128,2048]{1,0:T(8,128)(2,1)} %refs_0_.1), channel_id=1, source_target_pairs={{0,1},{1,0},{2,3},{3,2},{4,5},{5,4},{6,7},{7,6},{8,9},{9,8},{10,11... | collective-permute-start | bytes 1572872 | tf_op jit(solution)/shard_map/ppermute | solution.py:29
  0.5 1.9 %collective-permute-start.5 = (bf16[128,512]{1,0:T(8,128)(2,1)}, bf16[128,512]{1,0:T(8,128)(2,1)S(1)}, u32[]{:S(2)}, u32[]{:S(2)}) collective-permute-start(bf16[128,512]{1,0:T(8,128)(2,1)} %refs_1_.2), channel_id=1, source_target_pairs={{0,1},{1,0},{2,3},{3,2},{4,5},{5,4},{6,7},{7,6},{8,9},{9,8},{10,11... | collective-permute-start | bytes 393224 | tf_op jit(solution)/shard_map/ppermute | solution.py:29
  4.0 2.0 %collective-permute-start.6 = (bf16[512,512]{1,0:T(8,128)(2,1)S(1)}, bf16[512,512]{1,0:T(8,128)(2,1)S(1)}, u32[]{:S(2)}, u32[]{:S(2)}) collective-permute-start(bf16[512,512]{1,0:T(8,128)(2,1)S(1)} %get-tuple-element.56.own_ref), channel_id=1, source_target_pairs={{0,1},{1,0},{2,3},{3,2},{4,5},{5,4},{6,7},{7,6},{8,9},{9,8},{10,11... | collective-permute-start | bytes 1572872 | tf_op jit(solution)/shard_map/ppermute | solution.py:29
  9.0 4.4 %copy-start.2 = (s32[1,128]{1,0:T(1,128)S(1)}, s32[1,128]{1,0:T(1,128)}, u32[]{:S(2)}) copy-start(s32[1,128]{1,0:T(1,128)} %refs_1_.3) | copy-start | bytes 1540
  9.0 8.6 %collective-permute-start.17 = (bf16[256,256]{1,0:T(8,128)(2,1)S(1)}, bf16[256,256]{1,0:T(8,128)(2,1)S(1)}, u32[]{:S(2)}, u32[]{:S(2)}) collective-permute-start(bf16[256,256]{1,0:T(8,128)(2,1)S(1)} %get-tuple-element.76), channel_id=1, source_target_pairs={{0,8},{8,0},{16,24},{24,16},{1,9},{9,1},{17,25},{25,17},{2,10},{10... | collective-permute-start | bytes 393224 | tf_op jit(solution)/shard_map/ppermute | solution.py:29
  11.9 2.7 %copy-start.1 = (s32[4,8]{1,0:T(4,128)S(1)}, s32[4,8]{1,0:T(4,128)}, u32[]{:S(2)}) copy-start(s32[4,8]{1,0:T(4,128)} %new_ref.1) | copy-start | bytes 388
  11.9 2.7 %copy-start = (s32[4,4]{1,0:T(4,128)S(1)}, s32[4,4]{1,0:T(4,128)}, u32[]{:S(2)}) copy-start(s32[4,4]{1,0:T(4,128)} %old_ref.1) | copy-start | bytes 196
  11.9 7.4 %collective-permute-start.18 = (bf16[256,256]{1,0:T(8,128)(2,1)S(1)}, bf16[256,256]{1,0:T(8,128)(2,1)S(1)}, u32[]{:S(2)}, u32[]{:S(2)}) collective-permute-start(bf16[256,256]{1,0:T(8,128)(2,1)S(1)} %get-tuple-element.77), channel_id=1, source_target_pairs={{0,16},{8,24},{16,0},{24,8},{1,17},{9,25},{17,1},{25,9},{2,18},{10... | collective-permute-start | bytes 393224 | tf_op jit(solution)/shard_map/ppermute | solution.py:29
  13.5 1.2 %collective-permute-start.1 = (s32[1,128]{1,0:T(1,128)S(1)}, s32[1,128]{1,0:T(1,128)S(1)}, u32[]{:S(2)}, u32[]{:S(2)}) collective-permute-start(s32[1,128]{1,0:T(1,128)S(1)} %copy-done.2), channel_id=1, source_target_pairs={{0,1},{1,0},{2,3},{3,2},{4,5},{5,4},{6,7},{7,6},{8,9},{9,8},{10,11... | collective-permute-start | bytes 1544 | tf_op jit(solution)/shard_map/ppermute | solution.py:29
  13.5 7.7 %collective-permute-start.19 = (bf16[256,256]{1,0:T(8,128)(2,1)S(1)}, bf16[256,256]{1,0:T(8,128)(2,1)S(1)}, u32[]{:S(2)}, u32[]{:S(2)}) collective-permute-start(bf16[256,256]{1,0:T(8,128)(2,1)S(1)} %get-tuple-element.78), channel_id=1, source_target_pairs={{0,24},{8,16},{16,8},{24,0},{1,25},{9,17},{17,9},{25,1},{2,26},{10... | collective-permute-start | bytes 393224 | tf_op jit(solution)/shard_map/ppermute | solution.py:29
  15.6 7.0 %collective-permute-start.2 = (bf16[2,128,256]{2,1,0:T(8,128)(2,1)S(1)}, bf16[2,128,256]{2,1,0:T(8,128)(2,1)S(1)}, u32[]{:S(2)}, u32[]{:S(2)}) collective-permute-start(bf16[2,128,256]{2,1,0:T(8,128)(2,1)S(1)} %get-tuple-element.51), channel_id=1, source_target_pairs={{0,8},{8,0},{16,24},{24,16},{1,9},{9,1},{17,25},{25,17},{2,10},{10... | collective-permute-start | bytes 393224 | tf_op jit(solution)/shard_map/ppermute | solution.py:29
  16.5 9.0 %collective-permute-start.7 = (bf16[256,256]{1,0:T(8,128)(2,1)S(1)}, bf16[256,256]{1,0:T(8,128)(2,1)S(1)}, u32[]{:S(2)}, u32[]{:S(2)}) collective-permute-start(bf16[256,256]{1,0:T(8,128)(2,1)S(1)} %get-tuple-element.60), channel_id=1, source_target_pairs={{0,8},{8,0},{16,24},{24,16},{1,9},{9,1},{17,25},{25,17},{2,10},{10... | collective-permute-start | bytes 393224 | tf_op jit(solution)/shard_map/ppermute | solution.py:29
  17.7 9.3 %collective-permute-start.8 = (bf16[256,256]{1,0:T(8,128)(2,1)S(1)}, bf16[256,256]{1,0:T(8,128)(2,1)S(1)}, u32[]{:S(2)}, u32[]{:S(2)}) collective-permute-start(bf16[256,256]{1,0:T(8,128)(2,1)S(1)} %get-tuple-element.61), channel_id=1, source_target_pairs={{0,16},{8,24},{16,0},{24,8},{1,17},{9,25},{17,1},{25,9},{2,18},{10... | collective-permute-start | bytes 393224 | tf_op jit(solution)/shard_map/ppermute | solution.py:29
  19.4 10.2 %collective-permute-start.9 = (bf16[256,256]{1,0:T(8,128)(2,1)S(1)}, bf16[256,256]{1,0:T(8,128)(2,1)S(1)}, u32[]{:S(2)}, u32[]{:S(2)}) collective-permute-start(bf16[256,256]{1,0:T(8,128)(2,1)S(1)} %get-tuple-element.62), channel_id=1, source_target_pairs={{0,24},{8,16},{16,8},{24,0},{1,25},{9,17},{17,9},{25,1},{2,26},{10... | collective-permute-start | bytes 393224 | tf_op jit(solution)/shard_map/ppermute | solution.py:29
  21.1 11.8 %collective-permute-start.3 = (bf16[2,128,256]{2,1,0:T(8,128)(2,1)S(1)}, bf16[2,128,256]{2,1,0:T(8,128)(2,1)S(1)}, u32[]{:S(2)}, u32[]{:S(2)}) collective-permute-start(bf16[2,128,256]{2,1,0:T(8,128)(2,1)S(1)} %get-tuple-element.52), channel_id=1, source_target_pairs={{0,16},{8,24},{16,0},{24,8},{1,17},{9,25},{17,1},{25,9},{2,18},{10... | collective-permute-start | bytes 393224 | tf_op jit(solution)/shard_map/ppermute | solution.py:29
  22.6 10.9 %collective-permute-start.4 = (bf16[2,128,256]{2,1,0:T(8,128)(2,1)S(1)}, bf16[2,128,256]{2,1,0:T(8,128)(2,1)S(1)}, u32[]{:S(2)}, u32[]{:S(2)}) collective-permute-start(bf16[2,128,256]{2,1,0:T(8,128)(2,1)S(1)} %get-tuple-element.53), channel_id=1, source_target_pairs={{0,24},{8,16},{16,8},{24,0},{1,25},{9,17},{17,9},{25,1},{2,26},{10... | collective-permute-start | bytes 393224 | tf_op jit(solution)/shard_map/ppermute | solution.py:29
  25.4 10.6 %collective-permute-start.20 = (bf16[256,256]{1,0:T(8,128)(2,1)S(1)}, bf16[256,256]{1,0:T(8,128)(2,1)S(1)}, u32[]{:S(2)}, u32[]{:S(2)}) collective-permute-start(bf16[256,256]{1,0:T(8,128)(2,1)S(1)} %get-tuple-element.80), channel_id=1, source_target_pairs={{0,2},{1,3},{2,0},{3,1},{4,6},{5,7},{6,4},{7,5},{8,10},{9,11},{10,... | collective-permute-start | bytes 393224 | tf_op jit(solution)/shard_map/ppermute | solution.py:29
  27.0 11.6 %collective-permute-start.21 = (bf16[256,256]{1,0:T(8,128)(2,1)S(1)}, bf16[256,256]{1,0:T(8,128)(2,1)S(1)}, u32[]{:S(2)}, u32[]{:S(2)}) collective-permute-start(bf16[256,256]{1,0:T(8,128)(2,1)S(1)} %get-tuple-element.81), channel_id=1, source_target_pairs={{0,4},{1,5},{2,6},{3,7},{4,0},{5,1},{6,2},{7,3},{8,12},{9,13},{10,... | collective-permute-start | bytes 393224 | tf_op jit(solution)/shard_map/ppermute | solution.py:29
  29.6 9.8 %collective-permute-start.22 = (bf16[256,256]{1,0:T(8,128)(2,1)S(1)}, bf16[256,256]{1,0:T(8,128)(2,1)S(1)}, u32[]{:S(2)}, u32[]{:S(2)}) collective-permute-start(bf16[256,256]{1,0:T(8,128)(2,1)S(1)} %get-tuple-element.82), channel_id=1, source_target_pairs={{0,6},{1,7},{2,4},{3,5},{4,2},{5,3},{6,0},{7,1},{8,14},{9,15},{10,... | collective-permute-start | bytes 393224 | tf_op jit(solution)/shard_map/ppermute | solution.py:29
  32.9 7.1 %collective-permute-start.10 = (bf16[256,256]{1,0:T(8,128)(2,1)S(1)}, bf16[256,256]{1,0:T(8,128)(2,1)S(1)}, u32[]{:S(2)}, u32[]{:S(2)}) collective-permute-start(bf16[256,256]{1,0:T(8,128)(2,1)S(1)} %get-tuple-element.64), channel_id=1, source_target_pairs={{0,2},{1,3},{2,0},{3,1},{4,6},{5,7},{6,4},{7,5},{8,10},{9,11},{10,... | collective-permute-start | bytes 393224 | tf_op jit(solution)/shard_map/ppermute | solution.py:29
  33.5 16.8 %collective-permute-start.11 = (bf16[256,256]{1,0:T(8,128)(2,1)S(1)}, bf16[256,256]{1,0:T(8,128)(2,1)S(1)}, u32[]{:S(2)}, u32[]{:S(2)}) collective-permute-start(bf16[256,256]{1,0:T(8,128)(2,1)S(1)} %get-tuple-element.65), channel_id=1, source_target_pairs={{0,4},{1,5},{2,6},{3,7},{4,0},{5,1},{6,2},{7,3},{8,12},{9,13},{10,... | collective-permute-start | bytes 393224 | tf_op jit(solution)/shard_map/ppermute | solution.py:29
  36.1 14.2 %collective-permute-start.12 = (bf16[256,256]{1,0:T(8,128)(2,1)S(1)}, bf16[256,256]{1,0:T(8,128)(2,1)S(1)}, u32[]{:S(2)}, u32[]{:S(2)}) collective-permute-start(bf16[256,256]{1,0:T(8,128)(2,1)S(1)} %get-tuple-element.66), channel_id=1, source_target_pairs={{0,6},{1,7},{2,4},{3,5},{4,2},{5,3},{6,0},{7,1},{8,14},{9,15},{10,... | collective-permute-start | bytes 393224 | tf_op jit(solution)/shard_map/ppermute | solution.py:29
  39.8 10.9 %collective-permute-start.23 = (bf16[4,128,256]{2,1,0:T(8,128)(2,1)S(1)}, bf16[4,128,256]{2,1,0:T(8,128)(2,1)S(1)}, u32[]{:S(2)}, u32[]{:S(2)}) collective-permute-start(bf16[4,128,256]{2,1,0:T(8,128)(2,1)S(1)} %get-tuple-element.84), channel_id=1, source_target_pairs={{0,1},{1,0},{2,3},{3,2},{4,5},{5,4},{6,7},{7,6},{8,9},{9,8},{10,11... | collective-permute-start | bytes 786440 | tf_op jit(solution)/shard_map/ppermute | solution.py:29
  50.6 3.7 %collective-permute-start.13 = (bf16[4,128,256]{2,1,0:T(8,128)(2,1)S(1)}, bf16[4,128,256]{2,1,0:T(8,128)(2,1)S(1)}, u32[]{:S(2)}, u32[]{:S(2)}) collective-permute-start(bf16[4,128,256]{2,1,0:T(8,128)(2,1)S(1)} %get-tuple-element.68), channel_id=1, source_target_pairs={{0,1},{1,0},{2,3},{3,2},{4,5},{5,4},{6,7},{7,6},{8,9},{9,8},{10,11... | collective-permute-start | bytes 786440 | tf_op jit(solution)/shard_map/ppermute | solution.py:29
  50.8 6.4 %collective-permute-start.24 = (bf16[128,256]{1,0:T(8,128)(2,1)S(1)}, bf16[128,256]{1,0:T(8,128)(2,1)S(1)}, u32[]{:S(2)}, u32[]{:S(2)}) collective-permute-start(bf16[128,256]{1,0:T(8,128)(2,1)S(1)} %get-tuple-element.86), channel_id=1, source_target_pairs={{0,8},{8,0},{16,24},{24,16},{1,9},{9,1},{17,25},{25,17},{2,10},{10... | collective-permute-start | bytes 196616 | tf_op jit(solution)/shard_map/ppermute | solution.py:29
  51.8 6.1 %collective-permute-start.25 = (bf16[128,256]{1,0:T(8,128)(2,1)S(1)}, bf16[128,256]{1,0:T(8,128)(2,1)S(1)}, u32[]{:S(2)}, u32[]{:S(2)}) collective-permute-start(bf16[128,256]{1,0:T(8,128)(2,1)S(1)} %get-tuple-element.87), channel_id=1, source_target_pairs={{0,16},{8,24},{16,0},{24,8},{1,17},{9,25},{17,1},{25,9},{2,18},{10... | collective-permute-start | bytes 196616 | tf_op jit(solution)/shard_map/ppermute | solution.py:29
  53.6 5.7 %collective-permute-start.26 = (bf16[128,256]{1,0:T(8,128)(2,1)S(1)}, bf16[128,256]{1,0:T(8,128)(2,1)S(1)}, u32[]{:S(2)}, u32[]{:S(2)}) collective-permute-start(bf16[128,256]{1,0:T(8,128)(2,1)S(1)} %get-tuple-element.88), channel_id=1, source_target_pairs={{0,24},{8,16},{16,8},{24,0},{1,25},{9,17},{17,9},{25,1},{2,26},{10... | collective-permute-start | bytes 196616 | tf_op jit(solution)/shard_map/ppermute | solution.py:29
  54.4 4.9 %collective-permute-start.14 = (bf16[128,256]{1,0:T(8,128)(2,1)S(1)}, bf16[128,256]{1,0:T(8,128)(2,1)S(1)}, u32[]{:S(2)}, u32[]{:S(2)}) collective-permute-start(bf16[128,256]{1,0:T(8,128)(2,1)S(1)} %get-tuple-element.70), channel_id=1, source_target_pairs={{0,8},{8,0},{16,24},{24,16},{1,9},{9,1},{17,25},{25,17},{2,10},{10... | collective-permute-start | bytes 196616 | tf_op jit(solution)/shard_map/ppermute | solution.py:29
  55.4 4.6 %collective-permute-start.15 = (bf16[128,256]{1,0:T(8,128)(2,1)S(1)}, bf16[128,256]{1,0:T(8,128)(2,1)S(1)}, u32[]{:S(2)}, u32[]{:S(2)}) collective-permute-start(bf16[128,256]{1,0:T(8,128)(2,1)S(1)} %get-tuple-element.71), channel_id=1, source_target_pairs={{0,16},{8,24},{16,0},{24,8},{1,17},{9,25},{17,1},{25,9},{2,18},{10... | collective-permute-start | bytes 196616 | tf_op jit(solution)/shard_map/ppermute | solution.py:29
  57.2 5.2 %collective-permute-start.16 = (bf16[128,256]{1,0:T(8,128)(2,1)S(1)}, bf16[128,256]{1,0:T(8,128)(2,1)S(1)}, u32[]{:S(2)}, u32[]{:S(2)}) collective-permute-start(bf16[128,256]{1,0:T(8,128)(2,1)S(1)} %get-tuple-element.72), channel_id=1, source_target_pairs={{0,24},{8,16},{16,8},{24,0},{1,25},{9,17},{17,9},{25,1},{2,26},{10... | collective-permute-start | bytes 196616 | tf_op jit(solution)/shard_map/ppermute | solution.py:29
